TPU v7x, 256 devices: a whole 4x4x8 slice. The times are simulated.
256 devices in a mesh: frame: 32 (over x, z_hi, core), space: 8 (over z_lo, y).
Axes of the slice: x: 4, y: 4, z: 8 (z_hi: 4, z_lo: 2; z = z_hi * 2 + z_lo), core: 2. Of those that a mesh axis runs over, the one named last changes fastest.
Arguments:
- queries: bfloat16 [5120, 3072], P('frame', 'space'), may hold values from -24 to 24
- keys: bfloat16 [5120, 3072], P('frame', 'space'), may hold values from -24 to 24
- values: bfloat16 [5120, 3072], P('frame', 'space'), may hold values from -6 to 6
- grad_out: bfloat16 [5120, 3072], P('frame', 'space'), may hold values from -24 to 24
- proj_weight: bfloat16 [3072, 3072], P('space', 'frame'), may hold values from -0.109375 to 0.109375
Outputs:
- grad_queries: bfloat16 [5120, 3072], P('frame', 'space')
- grad_keys: bfloat16 [5120, 3072], P('frame', 'space')
- grad_values: bfloat16 [5120, 3072], P('frame', 'space')
- grad_proj: float32 [3072, 3072], P('space', 'frame')
All inputs are finite; a program needn't handle non-finite values.
Results may differ from a plain program's by a relative error of at most 0.03.
Values may be sent and summed in bfloat16 or wider, within the bound.
A program may use at most 64 MiB of HBM per device.

v0:
```python
import math

import jax
import jax.numpy as jnp
from jax import lax
from jax.sharding import PartitionSpec as P

HD = 128


def local(queries, keys, values, grad_out, proj_weight):
    tok_rows = queries.shape[0]
    width = queries.shape[1]
    heads_loc = width // HD
    factor = 1.0 / math.sqrt(HD)
    grad_rows = lax.all_gather(grad_out, "space", axis=1, tiled=True)
    grad_attn = lax.dot_general(
        grad_rows,
        lax.all_gather(proj_weight, "frame", axis=1, tiled=True),
        (((1,), (1,)), ((), ())),
        preferred_element_type=jnp.float32,
    ).astype(jnp.bfloat16)
    key_all, value_all = (
        lax.all_gather(keys, "frame", axis=0, tiled=True),
        lax.all_gather(values, "frame", axis=0, tiled=True),
    )
    seq_len = key_all.shape[0]
    key_block = math.gcd(seq_len, 512)
    nblocks = seq_len // key_block
    query3 = queries.reshape(tok_rows, heads_loc, HD)
    grad3 = grad_attn.reshape(tok_rows, heads_loc, HD)

    def block_of(source, offset, size):
        return lax.dynamic_slice_in_dim(source, offset, size, 0).reshape(size, heads_loc, HD)

    def scores_at(offset, size):
        key_blk = block_of(key_all, offset, size)
        logits = (
            jnp.einsum("qhd,khd->hqk", query3, key_blk, preferred_element_type=jnp.float32) * factor
        )
        return (logits, key_blk)

    def stats_step(index, carry):
        run_max, run_sum = carry
        logits, unused = scores_at(index * key_block, key_block)
        new_max = jnp.maximum(run_max, jnp.max(logits, axis=2))
        run_sum = run_sum * jnp.exp(run_max - new_max) + jnp.sum(
            jnp.exp(logits - new_max[:, :, None]), axis=2
        )
        return (new_max, run_sum)

    start_max = jnp.full((heads_loc, tok_rows), -jnp.inf, jnp.float32)
    start_sum = jnp.zeros((heads_loc, tok_rows), jnp.float32)
    run_max, run_sum = lax.fori_loop(0, nblocks, stats_step, (start_max, start_sum))
    log_norm = run_max + jnp.log(run_sum)

    def forward_step(index, accum):
        offset = index * key_block
        logits, unused = scores_at(offset, key_block)
        probs_low = jnp.exp(logits - log_norm[:, :, None]).astype(jnp.bfloat16)
        return accum + jnp.einsum(
            "hqk,khd->hqd",
            probs_low,
            block_of(value_all, offset, key_block),
            preferred_element_type=jnp.float32,
        )

    attn_acc = lax.fori_loop(
        0, nblocks, forward_step, jnp.zeros((heads_loc, tok_rows, HD), jnp.float32)
    )
    attn_out = attn_acc.astype(jnp.bfloat16)
    attn_rows = attn_out.transpose(1, 0, 2).reshape(tok_rows, width)
    row_delta = jnp.sum(
        grad3.astype(jnp.float32).transpose(1, 0, 2) * attn_out.astype(jnp.float32), axis=2
    )
    weight_term = lax.dot_general(
        attn_rows, grad_rows, (((0,), (0,)), ((), ())), preferred_element_type=jnp.float32
    )
    grad_proj = lax.psum_scatter(
        weight_term.astype(jnp.bfloat16), "frame", scatter_dimension=1, tiled=True
    ).astype(jnp.float32)

    def block_grads(offset, size):
        logits, key_blk = scores_at(offset, size)
        value_blk = block_of(value_all, offset, size)
        probs = jnp.exp(logits - log_norm[:, :, None])
        grad_probs = jnp.einsum(
            "qhd,khd->hqk", grad3, value_blk, preferred_element_type=jnp.float32
        )
        grad_logits = (probs * (grad_probs - row_delta[:, :, None])).astype(jnp.bfloat16)
        return (probs, grad_logits, key_blk)

    def key_value_rows(probs, grad_logits, size):
        value_grad = jnp.einsum(
            "hqk,qhd->khd", probs.astype(jnp.bfloat16), grad3, preferred_element_type=jnp.float32
        )
        key_grad = factor * jnp.einsum(
            "hqk,qhd->khd", grad_logits, query3, preferred_element_type=jnp.float32
        )
        return (
            key_grad.reshape(size, width).astype(jnp.bfloat16),
            value_grad.reshape(size, width).astype(jnp.bfloat16),
        )

    def backward_step(index, carry):
        grad_query, key_part, value_part = carry
        offset = index * key_block
        probs, grad_logits, key_blk = block_grads(offset, key_block)
        grad_query = grad_query + jnp.einsum(
            "hqk,khd->hqd", grad_logits, key_blk, preferred_element_type=jnp.float32
        )
        key_low, value_low = key_value_rows(probs, grad_logits, key_block)
        key_part = lax.dynamic_update_slice_in_dim(key_part, key_low, offset, 0)
        value_part = lax.dynamic_update_slice_in_dim(value_part, value_low, offset, 0)
        return (grad_query, key_part, value_part)

    start_query = jnp.zeros((heads_loc, tok_rows, HD), jnp.float32)
    start_part = jnp.zeros((seq_len, width), jnp.bfloat16)
    grad_query, key_part, value_part = lax.fori_loop(
        0, nblocks, backward_step, (start_query, start_part, start_part)
    )
    key_sum, value_sum = (
        lax.psum_scatter(
            key_part.astype(jnp.float32).astype(jnp.bfloat16),
            "frame",
            scatter_dimension=0,
            tiled=True,
        ).astype(jnp.float32),
        lax.psum_scatter(
            value_part.astype(jnp.float32).astype(jnp.bfloat16),
            "frame",
            scatter_dimension=0,
            tiled=True,
        ).astype(jnp.float32),
    )
    grad_keys = key_sum.astype(jnp.bfloat16)
    grad_values = value_sum.astype(jnp.bfloat16)
    grad_queries = (
        (factor * grad_query).transpose(1, 0, 2).reshape(tok_rows, width).astype(jnp.bfloat16)
    )
    return (grad_queries, grad_keys, grad_values, grad_proj)


def solution(mesh):
    in_specs = (
        P("frame", "space"),
        P("frame", "space"),
        P("frame", "space"),
        P("frame", "space"),
        P("space", "frame"),
    )
    out_specs = (P("frame", "space"), P("frame", "space"), P("frame", "space"), P("space", "frame"))
    return jax.shard_map(local, mesh=mesh, in_specs=in_specs, out_specs=out_specs, check_vma=False)
```

profile of v0, /device:TPU:8, one launch (start us, length us, event | category | flops | bytes accessed | tf_op | source)
XLA Modules:
  0.0 512.3 jit_solution(9974451108655350978)
XLA Ops:
  9.5 31.5 %all_gather.14 = bf16[160,3072]{1,0:T(8,128)(2,1)S(1)} all-gather(bf16[160,384]{1,0:T(8,128)(2,1)} %param.14), channel_id=1, replica_groups=mesh['frame'=32,'space'=8] {'space'}, dimensions={1}, use_global_device_ids=true | all-gather | bytes 1105920 | tf_op jit(solution)/shard_map/all_gather | solution.py:16
  41.0 27.0 %all-gather.8.cloned.1.call-done = bf16[384,3072]{0,1:T(8,128)(2,1)} async-done(((bf16[384,96]{0,1:T(8,128)(2,1)}), bf16[384,3072]{0,1:T(8,128)(2,1)}) %all-gather.8.cloned.1.call-update) | async-done | bytes 2359312 | tf_op jit(solution)/shard_map/all_gather | solution.py:19
  68.0 2.4 convolution_convert_fusion.2
  70.5 57.0 %all-gather.4.cloned.1.call-done = bf16[5120,384]{1,0:T(8,128)(2,1)} async-done(((bf16[160,384]{1,0:T(8,128)(2,1)}), bf16[5120,384]{1,0:T(8,128)(2,1)}) %all-gather.4.cloned.1.call-update) | async-done | bytes 3932176 | tf_op jit(solution)/shard_map/all_gather | solution.py:24
  127.5 6.3 %copy.41 = bf16[5120,384]{0,1:T(8,128)(2,1)} copy(bf16[5120,384]{1,0:T(8,128)(2,1)} %all-gather.4.cloned.1.call-done) | data formatting | bytes 7864320
  133.7 18.7 %while.48 = (s32[]{:T(128)}, f32[3,160]{1,0:T(4,128)S(1)}, f32[3,160]{1,0:T(4,128)S(1)}, bf16[5120,384]{0,1:T(8,128)(2,1)}, bf16[160,3,128]{2,0,1:T(8,128)(2,1)S...) while((s32[]{:T(128)}, f32[3,160]{1,0:T(4,128)S(1)}, f32[3,160]{1,0:T(4,128)S(1)}, ...), condition=%wide.region_3.0_spmd.clone, body=%wide.region_0.0_spmd.clone.sunk | while | flops 63900004 | bytes 3293730 | solution.py:54
  152.4 35.0 %all-gather.6.cloned.1.call-done = bf16[5120,384]{1,0:T(8,128)(2,1)} async-done(((bf16[160,384]{1,0:T(8,128)(2,1)}), bf16[5120,384]{1,0:T(8,128)(2,1)}) %all-gather.6.cloned.1.call-update) | async-done | bytes 3932176 | tf_op jit(solution)/shard_map/all_gather | solution.py:25
  187.4 6.3 %copy.43 = bf16[5120,384]{0,1:T(8,128)(2,1)} copy(bf16[5120,384]{1,0:T(8,128)(2,1)} %all-gather.6.cloned.1.call-done) | data formatting | bytes 7864320
  193.7 16.5 %while.49 = (s32[]{:T(128)}, f32[3,160,128]{2,1,0:T(8,128)S(1)}, bf16[5120,384]{0,1:T(8,128)(2,1)}, bf16[160,3,128]{2,0,1:T(8,128)(2,1)S(1)}, f32[3,160]{1,0:T(4...) while((s32[]{:T(128)}, f32[3,160,128]{2,1,0:T(8,128)S(1)}, ...), condition=%wide.region_5.0_spmd.clone, body=%wide.region_4.0_spmd.clone.sunk | while | flops 126689288 | bytes 2975785 | solution.py:68
  195.3 1.2 constant_dynamic-slice_fusion.10
  197.0 1.2 constant_dynamic-slice_fusion.10
  198.6 1.2 constant_dynamic-slice_fusion.10
  200.3 1.2 constant_dynamic-slice_fusion.10
  201.9 1.2 constant_dynamic-slice_fusion.10
  203.6 1.2 constant_dynamic-slice_fusion.10
  205.2 1.2 constant_dynamic-slice_fusion.10
  210.6 2.5 convolution_convert_fusion.1
  213.2 2.3 broadcast_in_dim.21.clone2
  215.4 2.3 broadcast_in_dim.21.clone
  217.7 50.4 %while.50 = (s32[]{:T(128)}, f32[3,160,128]{2,1,0:T(8,128)S(1)}, bf16[5120,384]{1,0:T(8,128)(2,1)}, bf16[5120,384]{1,0:T(8,128)(2,1)}, bf16[5120,384]{0,1:T(8,12...) while((s32[]{:T(128)}, f32[3,160,128]{2,1,0:T(8,128)S(1)}, ...), condition=%wide.region_8.0_spmd.clone, body=%wide.region_7.0_spmd.clone.sunk | while | flops 316760064 | bytes 12095441 | solution.py:119
  269.4 34.5 %reduce-scatter.8.cloned.1.call-done = bf16[384,96]{0,1:T(8,128)(2,1)} async-done(((bf16[384,3072]{0,1:T(8,128)(2,1)}), bf16[384,96]{0,1:T(8,128)(2,1)}) %reduce-scatter.8.cloned.1.call-update) | async-done | bytes 73744 | tf_op jit(solution)/shard_map/reduce_scatter | solution.py:79
  303.9 1.6 convert_element_type.87
  305.5 99.3 %reduce-scatter.6.cloned.1.call-done = bf16[160,384]{1,0:T(8,128)(2,1)} async-done(((bf16[5120,384]{1,0:T(8,128)(2,1)}), bf16[160,384]{1,0:T(8,128)(2,1)}) %reduce-scatter.6.cloned.1.call-update) | async-done | bytes 122896 | tf_op jit(solution)/shard_map/reduce_scatter | solution.py:129
  404.7 100.8 %reduce-scatter.4.cloned.1.call-done = bf16[160,384]{1,0:T(8,128)(2,1)} async-done(((bf16[5120,384]{1,0:T(8,128)(2,1)}), bf16[160,384]{1,0:T(8,128)(2,1)}) %reduce-scatter.4.cloned.1.call-update) | async-done | bytes 122896 | tf_op jit(solution)/shard_map/reduce_scatter | solution.py:123
  (197 shorter events, 80.1 us)
Async XLA Ops:
  7.2 63.3 %copy-start = (bf16[160,384]{1,0:T(8,128)(2,1)S(1)}, bf16[160,384]{1,0:T(8,128)(2,1)}, u32[]{:S(2)}) copy-start(bf16[160,384]{1,0:T(8,128)(2,1)} %param.11) | copy-start | bytes 368644
  7.2 60.8 %all-gather.8.cloned.1.call-start = ((), (), s32[]{:S(2)}) async-start(), calls=%async_computation.5 | async-start | bytes 2433024 | tf_op jit(solution)/shard_map/all_gather | solution.py:19
  7.9 119.6 %all-gather.4.cloned.1.call-start = ((), (), s32[]{:S(2)}) async-start(), calls=%async_computation.3 | async-start | bytes 4055040 | tf_op jit(solution)/shard_map/all_gather | solution.py:24
  8.7 178.8 %all-gather.6.cloned.1.call-start = ((), (), s32[]{:S(2)}) async-start(), calls=%async_computation.4 | async-start | bytes 4055040 | tf_op jit(solution)/shard_map/all_gather | solution.py:25
  9.4 294.5 %reduce-scatter.8.cloned.1.call-start = ((), (), s32[]{:S(2)}) async-start(), calls=%async_computation.8 | async-start | bytes 2433024 | tf_op jit(solution)/shard_map/reduce_scatter | solution.py:79
  213.1 191.6 %reduce-scatter.6.cloned.1.call-start = ((), (), s32[]{:S(2)}) async-start(), calls=%async_computation.7 | async-start | bytes 4055040 | tf_op jit(solution)/shard_map/reduce_scatter | solution.py:129
  268.1 237.4 %reduce-scatter.4.cloned.1.call-start = ((), (), s32[]{:S(2)}) async-start(), calls=%async_computation.6 | async-start | bytes 4055040 | tf_op jit(solution)/shard_map/reduce_scatter | solution.py:123
Sparse Core Ops, SparseCore 0:
  10.5 57.4 all-gather.7
  70.5 56.8 all-gather.3
  130.0 57.3 all-gather.5
  213.2 90.6 reduce-scatter.7
  308.3 96.3 reduce-scatter.5
  409.1 96.3 reduce-scatter.3
where the time goes:
time: 514 us; the launch traced here: 512 us
  waiting for transfers between devices  356 us (69%)
  local copies, waits for them, and re-layouts  73.9 us (14%)
  blocking collectives  31.5 us (6%)
  matrix products  28.4 us (6%)
  between operations  14.2 us (3%)
  other arithmetic  6.69 us (1%)
    reduce_scatter x1, waiting for transfers between devices, local(): lax.psum_scatter(key_part.astype(jnp.float32).astype(jnp.bfloat16), 'fram...  101 us
    reduce_scatter x1, waiting for transfers between devices, local(): lax.psum_scatter(value_part.astype(jnp.float32).astype(jnp.bfloat16), 'fr...  99.3 us
    all_gather x1, waiting for transfers between devices, local(): lax.all_gather(keys, 'frame', axis=0, tiled=True)  57 us
    dynamic_slice x40, local copies, waits for them, and re-layouts, block_of(): lax.dynamic_slice_in_dim(source, offset, size, 0)  42.6 us
    all_gather x1, waiting for transfers between devices, local(): lax.all_gather(values, 'frame', axis=0, tiled=True)  35 us
    reduce_scatter x1, waiting for transfers between devices, local(): lax.psum_scatter(weight_term.astype(jnp.bfloat16), 'frame', scatter_dimen...  34.5 us
    all_gather x1, blocking collectives, local(): grad_rows = lax.all_gather(grad_out, 'space', axis=1, tiled=True)  31.5 us
    all_gather x1, waiting for transfers between devices, local(): lax.all_gather(proj_weight, 'frame', axis=1, tiled=True)  27 us
  transfers between devices with their start and end apart: 6, of which 6 were waited for; matrix products, arithmetic and copies ran while one was open for 16% of the time, Pallas kernels for 0%

commit v1 on v0

v1 whole, which is shorter than its diff:
```python
import math

import jax
import jax.numpy as jnp
from jax import lax
from jax.experimental import pallas as pl
from jax.experimental.pallas import tpu as pltpu
from jax.sharding import PartitionSpec as P

HD = 128
MESH = pl.DeviceIdType.MESH
F32 = jnp.float32
BF16 = jnp.bfloat16
RING = 4
CORES = 2
PAIR = 2


def mm(a, b):
    return jnp.dot(a, b, preferred_element_type=F32)


def kernel(dims, q_ref, k_ref, v_ref, g_ref, w_ref, dq_ref, dk_ref, dv_ref, gp_ref, *scratch):
    rows, heads, wcols, nsem = dims
    (q4, k8, v8, g8, wb, da, do4, qt, kt, vt, dot_, don, s_buf, p_buf, ot, st_out, st_in,
     ob, ol, dqt, dqb, dql, dkb, dvb, dkc, dvc, dkl, dvl, gpb, gpc, gpx, gpz, gpr,
     send_sems, recv_sems) = scratch
    width = heads * HD
    nq = RING * rows
    kc = CORES * rows
    factor = 1.0 / math.sqrt(HD)
    c2 = factor * math.log2(math.e)

    f = lax.axis_index("frame")
    s = lax.axis_index("space")
    x, zh, core = f // 8, lax.rem(f // 2, 4), lax.rem(f, 2)
    zl, y = s // 4, lax.rem(s, 4)

    def around(i, k):
        return lax.rem(i + k, RING)

    def dev_f(xx, zz, cc):
        return {"frame": (xx * RING + zz) * CORES + cc}

    xs = [dev_f(around(x, k), zh, core) for k in range(4)]
    zs = [dev_f(x, around(zh, k), core) for k in range(4)]
    sib = dev_f(x, zh, 1 - core)
    ys = [{"space": zl * RING + around(y, k)} for k in range(4)]
    zsib = {"space": (1 - zl) * RING + y}

    partners = [zs[1], zs[2], zs[3], xs[1], xs[3], ys[1], ys[3], sib, zsib]
    barrier = pltpu.get_barrier_semaphore()
    for other in partners:
        pl.semaphore_signal(barrier, inc=1, device_id=other, device_id_type=MESH)
    pl.semaphore_wait(barrier, len(partners))

    used = [0]
    pending = []

    def send(src, dst, device):
        n = used[0]
        used[0] += 1
        copy = pltpu.make_async_remote_copy(
            src_ref=src, dst_ref=dst, send_sem=send_sems.at[n], recv_sem=recv_sems.at[n],
            device_id=device, device_id_type=MESH)
        copy.start()
        pending.append(copy)
        return copy

    def gather(own, at, lo, hi, i, devs, forward=None):
        p, n, o = around(i, 1), around(i, 3), around(i, 2)
        c0 = send(own, at(i), devs[1])
        c1 = send(own, at(i), devs[3])
        fw = []
        if forward is not None:
            fw.append(send(own, at(i), forward))
        yield
        c0.wait_recv()
        c2 = send(lo(n), lo(n), devs[1])
        if forward is not None:
            fw.append(send(at(n), at(n), forward))
        c1.wait_recv()
        c3 = send(hi(p), hi(p), devs[3])
        if forward is not None:
            fw.append(send(at(p), at(p), forward))
        yield
        c2.wait_recv()
        c3.wait_recv()
        if forward is not None:
            fw.append(send(at(o), at(o), forward))
            yield
            for c in fw:
                c.wait_recv()

    def add_into(dst, landed):
        dst[...] = (dst[...].astype(F32) + landed[...].astype(F32)).astype(BF16)

    def scatter(blk, size, land, i, devs, out):
        h = size // 2
        p, n, o = around(i, 1), around(i, 3), around(i, 2)
        a0, b0 = land.at[0, 0:h], land.at[0, h:size]
        from_n, from_p = land.at[1], land.at[2]
        c0 = send(blk(o, 0, h), a0, devs[1])
        c1 = send(blk(o, h, size), b0, devs[3])
        c2 = send(blk(p, h, size), land.at[1, h:size], devs[1])
        c3 = send(blk(n, 0, h), land.at[2, 0:h], devs[3])
        yield
        c0.wait_recv()
        add_into(blk(p, 0, h), a0)
        c4 = send(blk(p, 0, h), land.at[1, 0:h], devs[1])
        c1.wait_recv()
        add_into(blk(n, h, size), b0)
        c5 = send(blk(n, h, size), land.at[2, h:size], devs[3])
        yield
        for c in (c2, c3, c4, c5):
            c.wait_recv()
        out(blk(i, 0, size)[...].astype(F32) + from_n[...].astype(F32) + from_p[...].astype(F32))

    def pump(*flows):
        for flow in flows:
            next(flow, None)

    half = rows // 2
    wz = gather(w_ref, lambda j: wb.at[x, j, core], lambda j: wb.at[x, j, core, 0:wcols // 2],
                lambda j: wb.at[x, j, core, wcols // 2:wcols], zh, zs)
    qz = gather(q_ref, lambda j: q4.at[j], lambda j: q4.at[j, 0:half],
                lambda j: q4.at[j, half:rows], zh, zs)
    kx = gather(k_ref, lambda j: k8.at[j, core], lambda j: k8.at[j, core, 0:half],
                lambda j: k8.at[j, core, half:rows], x, xs, sib)
    vx = gather(v_ref, lambda j: v8.at[j, core], lambda j: v8.at[j, core, 0:half],
                lambda j: v8.at[j, core, half:rows], x, xs, sib)
    pump(wz)
    gz = send(g_ref, g8.at[zl, y], zsib)
    pump(kx, qz, vx)
    g8[zl, y] = g_ref[...]
    wb[x, zh, core] = w_ref[...]
    q4[zh] = q_ref[...]
    k8[x, core] = k_ref[...]
    v8[x, core] = v_ref[...]

    gz.wait_recv()
    gy = gather(g8.at[:, y], lambda j: g8.at[:, j], lambda j: g8.at[0, j],
                lambda j: g8.at[1, j], y, ys)
    pump(gy)
    pump(wz, kx, qz)
    pump(wz)
    wx = gather(wb.at[x, :, core], lambda j: wb.at[j, :, core], lambda j: wb.at[j, 0:2, core],
                lambda j: wb.at[j, 2:4, core], x, xs, sib)
    pump(wx)
    pump(vx, gy, kx, qz, kx)

    def cols(h):
        return slice(h * HD, (h + 1) * HD)

    for h in range(heads):
        qt[h] = q4[:, :, cols(h)].reshape(nq, HD).T
    for h in range(heads):
        for j in range(RING):
            kt[h, j] = k8[j, :, :, cols(h)].reshape(kc, HD).T

    st_out[...] = jnp.zeros_like(st_out)

    def logits_pass(h):
        def body(j, m8):
            sc = mm(k8[j, :, :, cols(h)].reshape(kc, HD), qt[h])
            s_buf[j] = sc
            return jnp.maximum(m8, jnp.max(sc.reshape(kc // 8, 8, nq), axis=0))
        m8 = lax.fori_loop(0, RING, body, jnp.full((8, nq), -jnp.inf, F32))
        return jnp.max(m8, axis=0, keepdims=True)

    def probs_pass(h, m):
        ot[h] = jnp.zeros((HD, nq), F32)

        def body(j, l8):
            pr = jnp.exp2((s_buf[j] - m) * c2)
            low = pr.astype(BF16)
            p_buf[h, j] = low
            ot[h] += mm(vt[h, j], low)
            return l8 + jnp.sum(pr.reshape(kc // 8, 8, nq), axis=0)
        l8 = lax.fori_loop(0, RING, body, jnp.zeros((8, nq), F32))
        st_out[h:h + 1] = m
        st_out[8 + h:9 + h] = jnp.sum(l8, axis=0, keepdims=True)

    m = logits_pass(0)
    pump(wx, vx, vx)
    for h in range(heads):
        for j in range(RING):
            vt[h, j] = v8[j, :, :, cols(h)].reshape(kc, HD).T
    probs_pass(0, m)
    pump(wx, gy)
    for h in range(1, heads - 1):
        probs_pass(h, logits_pass(h))
    pump(wx)

    acc = jnp.zeros((rows, width), F32)
    for t in range(PAIR * RING):
        block = wb[t // 2, 2 * (t % 2):2 * (t % 2) + 2].reshape(width, width)
        acc = acc + mm(g8[t // RING, t % RING], block)
    da[...] = acc.astype(BF16)
    dz = gather(da, lambda j: do4.at[j], lambda j: do4.at[j, 0:half],
                lambda j: do4.at[j, half:rows], zh, zs)
    pump(dz)
    do4[zh] = da[...]
    m = logits_pass(heads - 1)
    pump(dz)
    probs_pass(heads - 1, m)
    pump(dz)

    for h in range(heads):
        dt = do4[:, :, cols(h)].reshape(nq, HD).astype(F32).T
        dot_[h] = dt
        st_out[16 + h:17 + h] = jnp.sum(dt * ot[h], axis=0, keepdims=True)

    st = [send(st_out, st_in.at[zh], zs[k]) for k in (1, 2, 3)]
    for c in st:
        c.wait_recv()
    st_in[zh] = st_out[...]
    ms = [st_in[j, 0:8] for j in range(RING)]
    m_all = jnp.maximum(jnp.maximum(ms[0], ms[1]), jnp.maximum(ms[2], ms[3]))
    es = [jnp.exp2((mj - m_all) * c2) for mj in ms]
    l_all = sum(es[j] * st_in[j, 8:16] for j in range(RING))
    u_all = sum(es[j] * st_in[j, 16:24] for j in range(RING))
    inv = 1.0 / jnp.where(l_all > 0.0, l_all, 1.0)
    scale = jnp.exp2((st_out[0:8] - m_all) * c2) * inv
    delta = u_all * inv * scale

    for h in range(heads):
        o_n = (ot[h] * scale[h:h + 1]).T
        ob[:, :, cols(h)] = o_n.astype(BF16).reshape(RING, rows, HD)
    attn = {}

    def keep_attn(value):
        attn["out"] = value.astype(BF16)

    oz = scatter(lambda j, lo, hi: ob.at[j, lo:hi], rows, ol, zh, zs, keep_attn)
    pump(oz)

    def backward(h):
        ds_h = dot_[h] * scale[h:h + 1]
        dsl = ds_h.astype(BF16)
        don[...] = ds_h.T.astype(BF16)
        dl = delta[h:h + 1]
        dqt[...] = jnp.zeros_like(dqt)

        def body(j, unused):
            dp = mm(v8[j, :, :, cols(h)].reshape(kc, HD), dsl)
            pr = p_buf[h, j]
            dlog = (pr.astype(F32) * (dp - dl)).astype(BF16)
            dvb[h, :, j] = mm(pr, don[...]).astype(BF16).reshape(CORES, rows, HD)
            dkb[h, :, j] = (factor * mm(dlog, q4[:, :, cols(h)].reshape(nq, HD))).astype(
                BF16).reshape(CORES, rows, HD)
            dqt[...] += mm(kt[h, j], dlog)
            return unused
        lax.fori_loop(0, RING, body, 0)
        dqb[h] = (factor * dqt[...]).T.astype(BF16).reshape(RING, rows, HD)

    def pair_then_ring(part, landc, land, h, out):
        c = send(part.at[h, 1 - core], landc.at[h], sib)
        yield
        c.wait_recv()
        mine = part.at[h, core]
        add_into(mine, landc.at[h])
        ring = scatter(lambda j, lo, hi: part.at[h, core, j, lo:hi], rows, land.at[h], x, xs, out)
        yield from ring

    def writer(ref, h):
        def write(value):
            ref[:, cols(h)] = value.astype(BF16)
        return write

    flows = []

    def exits(h):
        return [pair_then_ring(dkb, dkc, dkl, h, writer(dk_ref, h)),
                pair_then_ring(dvb, dvc, dvl, h, writer(dv_ref, h)),
                scatter(lambda j, lo, hi: dqb.at[h, j, lo:hi], rows, dql.at[h], zh, zs,
                        writer(dq_ref, h))]

    backward(0)
    flows.append(exits(0))
    pump(*flows[0])
    pump(oz, *flows[0][:2])
    backward(1)
    flows.append(exits(1))
    pump(*flows[1])
    pump(oz, *flows[0])
    pump(*flows[1][:2])

    out_low = attn["out"]
    for t in range(PAIR * RING):
        part = lax.dot_general(g8[t // RING, t % RING], out_low, (((0,), (0,)), ((), ())),
                               preferred_element_type=F32)
        gpb[t // 2, 2 * (t % 2):2 * (t % 2) + 2] = part.astype(BF16).reshape(
            2, CORES, wcols, width)

    def proj_flow():
        c = send(gpb.at[:, :, 1 - core], gpc, sib)
        yield
        c.wait_recv()
        for j in range(RING):
            add_into(gpb.at[j, :, core], gpc.at[j])

        def keep(value):
            gpr[...] = value.astype(BF16)
        yield from scatter(lambda j, lo, hi: gpb.at[j, lo:hi, core], RING, gpx, x, xs, keep)

        def final(value):
            gp_ref[...] = value
        yield from scatter(lambda j, lo, hi: gpr.at[j, lo:hi], wcols, gpz, zh, zs, final)

    gpf = proj_flow()
    pump(gpf)
    backward(2)
    flows.append(exits(2))
    pump(gpf)
    pump(*flows[2])
    for fl in flows[0]:
        pump(fl)
    for fl in flows[1]:
        pump(fl)
    pump(gpf)
    live = flows[2] + flows[1] + flows[0] + [gpf]
    while live:
        live = [fl for fl in live if next(fl, True) is None]
    for c in pending:
        c.wait_send()
    assert used[0] <= nsem, used[0]


def local(queries, keys, values, grad_out, proj_weight):
    rows, width = queries.shape
    heads = width // HD
    wcols = proj_weight.shape[1]
    nq, kc = RING * rows, CORES * rows
    nsem = 144

    def vm(*shape, dtype=BF16):
        return pltpu.VMEM(shape, dtype)

    scratch = [
        vm(RING, rows, width), vm(RING, CORES, rows, width), vm(RING, CORES, rows, width),
        vm(PAIR, RING, rows, width), vm(RING, RING, CORES, wcols, width),
        vm(rows, width), vm(RING, rows, width),
        vm(heads, HD, nq), vm(heads, RING, HD, kc), vm(heads, RING, HD, kc),
        vm(heads, HD, nq, dtype=F32), vm(nq, HD),
        vm(RING, kc, nq, dtype=F32), vm(heads, RING, kc, nq), vm(heads, HD, nq, dtype=F32),
        vm(24, nq, dtype=F32), vm(RING, 24, nq, dtype=F32),
        vm(RING, rows, width), vm(3, rows, width),
        vm(HD, nq, dtype=F32), vm(heads, RING, rows, HD), vm(heads, 3, rows, HD),
        vm(heads, CORES, RING, rows, HD), vm(heads, CORES, RING, rows, HD),
        vm(heads, RING, rows, HD), vm(heads, RING, rows, HD),
        vm(heads, 3, rows, HD), vm(heads, 3, rows, HD),
        vm(RING, RING, CORES, wcols, width), vm(RING, RING, wcols, width),
        vm(3, RING, wcols, width), vm(3, wcols, width), vm(RING, wcols, width),
        pltpu.SemaphoreType.DMA((nsem,)), pltpu.SemaphoreType.DMA((nsem,)),
    ]
    vmem = pl.BlockSpec(memory_space=pltpu.VMEM)

    def body(*refs):
        kernel((rows, heads, wcols, nsem), *refs)

    like = jax.ShapeDtypeStruct((rows, width), BF16)
    dq, dk, dv, gp = pl.pallas_call(
        body,
        out_shape=(like, like, like, jax.ShapeDtypeStruct((wcols, width), F32)),
        in_specs=[vmem] * 5,
        out_specs=(vmem,) * 4,
        scratch_shapes=scratch,
        compiler_params=pltpu.CompilerParams(
            collective_id=0, has_side_effects=True, vmem_limit_bytes=60 * 1024 * 1024),
        name="fused",
    )(queries, keys, values, grad_out, proj_weight.T)
    return dq, dk, dv, gp.T


def solution(mesh):
    spec = P("frame", "space")
    return jax.shard_map(
        local, mesh=mesh, in_specs=(spec,) * 4 + (P("space", "frame"),),
        out_specs=(spec,) * 3 + (P("space", "frame"),), check_vma=False)
```

time: 514 us -> 113 us (0.22)
  waiting for transfers between devices: 356 us -> 0 us
  Pallas kernels: 0 us -> 108 us
  local copies, waits for them, and re-layouts: 73.9 us -> 4.16 us
  blocking collectives: 31.5 us -> 0 us
  matrix products: 28.4 us -> 0 us
  between operations: 14.2 us -> 0.65 us
  other arithmetic: 6.69 us -> 0 us
    reduce_scatter x3 -> x0, waiting for transfers between devices: 235 us -> none  [the longest x1 101 us: local(): lax.psum_scatter(key_part.astype(jnp.float32).astype(jnp.bfloat16), 'fram...]
    all_gather x3 -> x0, waiting for transfers between devices: 119 us -> none  [the longest x1 57 us: local(): lax.all_gather(keys, 'frame', axis=0, tiled=True)]
    pallas_call x0 -> x1, Pallas kernels: none -> 108 us  [local(): pl.pallas_call(body, out_shape=(like, like, like, jax.ShapeDtypeStruct((w...]
    dynamic_slice x40 -> x0, local copies, waits for them, and re-layouts: 42.6 us -> none  [block_of(): lax.dynamic_slice_in_dim(source, offset, size, 0)]
    all_gather x1 -> x0, blocking collectives: 31.5 us -> none  [local(): grad_rows = lax.all_gather(grad_out, 'space', axis=1, tiled=True)]
    dot_general x72 -> x0, matrix products: 28.4 us -> none  [the longest x20 6.87 us: scores_at(): jnp.einsum('qhd,khd->hqk', query3, key_blk, preferred_element_type=jnp.fl...]
    dynamic_update_slice x30 -> x0, local copies, waits for them, and re-layouts: 14 us -> none  [the longest x20 11.9 us: backward_step(): lax.dynamic_update_slice_in_dim(value_part, value_low, offset, 0)]
    unnamed x6 -> x10, local copies, waits for them, and re-layouts: 12.7 us -> 4.16 us
  transfers between devices with their start and end apart: 6 -> 0, of which waited for: 6 -> 0; matrix products, arithmetic and copies ran while one was open for 16% -> 0% of each run, Pallas kernels for 0% -> 0%
where the time goes in v1:
time: 113 us
  Pallas kernels  108 us (96%)
  local copies, waits for them, and re-layouts  4.16 us (4%)
    pallas_call x1, Pallas kernels, local(): pl.pallas_call(body, out_shape=(like, like, like, jax.ShapeDtypeStruct((w...  108 us
    unnamed x10, local copies, waits for them, and re-layouts  4.16 us

profile of v1, /device:TPU:8, one launch (start us, length us, event | category | flops | bytes accessed | tf_op | source)
XLA Modules:
  0.0 112.5 jit_solution(3677339531845373616)
XLA Ops:
  0.6 107.7 %fused.1 = (bf16[160,384]{1,0:T(8,128)(2,1)}, bf16[160,384]{1,0:T(8,128)(2,1)}, bf16[160,384]{1,0:T(8,128)(2,1)}, f32[96,384]{1,0:T(8,128)}) custom-call(bf16[160,384]{1,0:T(8,128)(2,1)} %refs_0_.1, bf16[160,384]{1,0:T(8,128)(2,1)} %refs_1_.1, bf16[160,384]{1,0:T(8,128)(2,1)} %refs_2_.1, bf16[160,384]{1,0:T(8,128)(2,1)} %refs_3_.1, bf16[96,384]{1,0:T(8,128)(2,1)} %bitcast.3), custom_call_target="tpu_custom_call" | custom-call | tf_op jit(solution)/shard_map/fused/pallas_call | solution.py:363
  108.3 0.0 copy-start.2
  108.4 1.6 %copy.13 = bf16[160,384]{1,0:T(8,128)(2,1)} copy(bf16[160,384]{1,0:T(8,128)(2,1)} %get-tuple-element.16) | data formatting | bytes 245760
  110.0 0.0 copy-done.2
  110.0 0.0 copy-start.1
  110.0 0.6 copy.14
  110.6 0.3 copy-done.1
  110.9 0.0 copy-start
  110.9 0.6 copy.15
  111.6 0.3 copy-done
  111.9 0.7 copy.16
Async XLA Ops:
  108.3 1.6 %copy-start.2 = (bf16[160,384]{1,0:T(8,128)(2,1)S(1)}, bf16[160,384]{1,0:T(8,128)(2,1)}, u32[]{:S(2)}) copy-start(bf16[160,384]{1,0:T(8,128)(2,1)} %get-tuple-element.17) | copy-start | bytes 368644
  110.0 0.9 copy-start.1
  110.9 1.0 copy-start

commit v2 on v1

v2 whole, which is shorter than its diff:
```python
import math

import jax
import jax.numpy as jnp
from jax import lax
from jax.experimental import pallas as pl
from jax.experimental.pallas import tpu as pltpu
from jax.sharding import PartitionSpec as P

HD = 128
MESH = pl.DeviceIdType.MESH
F32 = jnp.float32
BF16 = jnp.bfloat16
RING = 4
CORES = 2
PAIR = 2


def mm(a, b):
    return jnp.dot(a, b, preferred_element_type=F32)


def kernel(dims, q_ref, k_ref, v_ref, g_ref, w_ref, dq_ref, dk_ref, dv_ref, gp_ref, *scratch):
    rows, heads, wcols, nsem = dims
    (q4, kv8, g8, gt, wb, da, do4, qt, kt, vt, don, s_buf, p_buf, ot, l_in, u_out, l_out, u_in,
     ob, ol, dqt, dqb, dql, dkvb, dkvc, dkvl, gpb, gpc, gpx, gpz, gpr,
     send_sems, recv_sems) = scratch
    width = heads * HD
    nq = RING * rows
    kc = CORES * rows
    factor = 1.0 / math.sqrt(HD)
    c2 = factor * math.log2(math.e)

    f = lax.axis_index("frame")
    s = lax.axis_index("space")
    x, zh, core = f // 8, lax.rem(f // 2, 4), lax.rem(f, 2)
    zl, y = s // 4, lax.rem(s, 4)

    def around(i, k):
        return lax.rem(i + k, RING)

    def dev_f(xx, zz, cc):
        return {"frame": (xx * RING + zz) * CORES + cc}

    xs = [dev_f(around(x, k), zh, core) for k in range(4)]
    zs = [dev_f(x, around(zh, k), core) for k in range(4)]
    sib = dev_f(x, zh, 1 - core)
    ys = [{"space": zl * RING + around(y, k)} for k in range(4)]
    zsib = {"space": (1 - zl) * RING + y}

    partners = [zs[1], zs[3], xs[1], xs[3], ys[1], ys[3], sib, zsib]
    barrier = pltpu.get_barrier_semaphore()
    for other in partners:
        pl.semaphore_signal(barrier, inc=1, device_id=other, device_id_type=MESH)
    pl.semaphore_wait(barrier, len(partners))

    used = [0]
    pending = []

    def send(src, dst, device):
        n = used[0]
        used[0] += 1
        copy = pltpu.make_async_remote_copy(
            src_ref=src, dst_ref=dst, send_sem=send_sems.at[n], recv_sem=recv_sems.at[n],
            device_id=device, device_id_type=MESH)
        copy.start()
        pending.append(copy)
        return copy

    def gather(own, at, lo, hi, i, devs, forward=None):
        p, n, o = around(i, 1), around(i, 3), around(i, 2)
        first = [(send(src, dst, devs[1]), send(src, dst, devs[3])) for src, dst in own]
        fw = []
        if forward is not None:
            fw += [send(src, dst, forward) for src, dst in own]
        yield
        for c0, _ in first:
            c0.wait_recv()
        c2 = send(lo(n), lo(n), devs[1])
        if forward is not None:
            fw.append(send(at(n), at(n), forward))
        for _, c1 in first:
            c1.wait_recv()
        c3 = send(hi(p), hi(p), devs[3])
        if forward is not None:
            fw.append(send(at(p), at(p), forward))
        yield
        c2.wait_recv()
        c3.wait_recv()
        if forward is not None:
            fw.append(send(at(o), at(o), forward))
            yield
            for c in fw:
                c.wait_recv()

    def add_into(dst, landed):
        dst[...] = (dst[...].astype(F32) + landed[...].astype(F32)).astype(BF16)

    def scatter(blk, size, land, i, devs, out):
        h = size // 2
        p, n, o = around(i, 1), around(i, 3), around(i, 2)
        a0, b0 = land.at[0, 0:h], land.at[0, h:size]
        from_n, from_p = land.at[1], land.at[2]
        c0 = send(blk(o, 0, h), a0, devs[1])
        c1 = send(blk(o, h, size), b0, devs[3])
        c2 = send(blk(p, h, size), land.at[1, h:size], devs[1])
        c3 = send(blk(n, 0, h), land.at[2, 0:h], devs[3])
        yield
        c0.wait_recv()
        add_into(blk(p, 0, h), a0)
        c4 = send(blk(p, 0, h), land.at[1, 0:h], devs[1])
        c1.wait_recv()
        add_into(blk(n, h, size), b0)
        c5 = send(blk(n, h, size), land.at[2, h:size], devs[3])
        yield
        for c in (c2, c3, c4, c5):
            c.wait_recv()
        out(blk(i, 0, size)[...].astype(F32) + from_n[...].astype(F32) + from_p[...].astype(F32))

    def spread(src, land):
        copies = [send(src, land.at[zh], zs[k]) for k in (1, 3, 2)]
        yield
        for c in copies:
            c.wait_recv()

    def pump(*flows):
        for flow in flows:
            next(flow, None)

    def cols(h):
        return slice(h * HD, (h + 1) * HD)

    half = rows // 2
    hw = wcols // 2
    H = range(heads)

    def q_flow(h):
        own = [(q_ref.at[:, cols(h)], q4.at[h, zh])]
        return gather(own, lambda j: q4.at[h, j], lambda j: q4.at[h, j, 0:half],
                      lambda j: q4.at[h, j, half:rows], zh, zs)

    def kv_flow(h):
        own = [(k_ref.at[:, cols(h)], kv8.at[h, x, core, 0]),
               (v_ref.at[:, cols(h)], kv8.at[h, x, core, 1])]
        return gather(own, lambda j: kv8.at[h, j, core], lambda j: kv8.at[h, j, core, 0],
                      lambda j: kv8.at[h, j, core, 1], x, xs, sib)

    def wz_flow(h):
        own = [(w_ref.at[:, cols(h)], wb.at[h, x, zh, core])]
        return gather(own, lambda j: wb.at[h, x, j, core], lambda j: wb.at[h, x, j, core, 0:hw],
                      lambda j: wb.at[h, x, j, core, hw:wcols], zh, zs)

    def wx_flow(h):
        own = [(wb.at[h, x, :, core], wb.at[h, x, :, core])]
        return gather(own, lambda j: wb.at[h, j, :, core], lambda j: wb.at[h, j, 0:2, core],
                      lambda j: wb.at[h, j, 2:4, core], x, xs, sib)

    def g_flow():
        c = send(g_ref, g8.at[zl, y], zsib)
        yield
        c.wait_recv()
        own = [(g8.at[:, y], g8.at[:, y])]
        yield from gather(own, lambda j: g8.at[:, j], lambda j: g8.at[0, j],
                          lambda j: g8.at[1, j], y, ys)

    def do_flow(h):
        own = [(da.at[h], do4.at[h, zh])]
        return gather(own, lambda j: do4.at[h, j], lambda j: do4.at[h, j, 0:half],
                      lambda j: do4.at[h, j, half:rows], zh, zs)

    def turn(h):
        qt[h] = q4[h].reshape(nq, HD).T
        for j in range(RING):
            kt[h, j] = kv8[h, j, :, 0].reshape(kc, HD).T
            vt[h, j] = kv8[h, j, :, 1].reshape(kc, HD).T

    def logits_pass(h):
        def body(j, m8):
            sc = mm(kv8[h, j, :, 0].reshape(kc, HD), qt[h])
            s_buf[j] = sc
            return jnp.maximum(m8, jnp.max(sc.reshape(kc // 8, 8, nq), axis=0))
        m8 = lax.fori_loop(0, RING, body, jnp.full((8, nq), -jnp.inf, F32))
        return jnp.max(m8, axis=0, keepdims=True)

    def probs_pass(h, m):
        ot[h] = jnp.zeros((HD, nq), F32)

        def body(j, l8):
            pr = jnp.exp2((s_buf[j] - m) * c2)
            low = pr.astype(BF16)
            p_buf[h, j] = low
            ot[h] += mm(vt[h, j], low)
            return l8 + jnp.sum(pr.reshape(kc // 8, 8, nq), axis=0)
        l8 = lax.fori_loop(0, RING, body, jnp.zeros((8, nq), F32))
        l_out[h] = m * c2 + jnp.log2(jnp.sum(l8, axis=0, keepdims=True))

    scales = {}

    def normalise(h, m):
        l_in[h, zh] = l_out[h]
        ls = [l_in[h, j] for j in range(RING)]
        top = jnp.maximum(jnp.maximum(ls[0], ls[1]), jnp.maximum(ls[2], ls[3]))
        total = sum(jnp.exp2(v - top) for v in ls)
        scales[h] = jnp.exp2(m * c2 - (top + jnp.log2(total)))
        ob[h] = (ot[h] * scales[h]).T.astype(BF16).reshape(RING, rows, HD)

    attn = {}

    def o_flow(h):
        def keep(value):
            attn[h] = value.astype(BF16)
        return scatter(lambda j, lo, hi: ob.at[h, j, lo:hi], rows, ol.at[h], zh, zs, keep)

    def grad_attn(h):
        acc = jnp.zeros((rows, HD), F32)
        for t in range(PAIR * RING):
            block = wb[h, t // 2, 2 * (t % 2):2 * (t % 2) + 2].reshape(width, HD)
            acc = acc + mm(g8[t // RING, t % RING], block)
        low = acc.astype(BF16)
        da[h] = low
        do4[h, zh] = low

    grads = {}

    def row_terms(h):
        scaled = do4[h].reshape(nq, HD).astype(F32).T * scales[h]
        u_out[h] = jnp.sum(scaled * ot[h], axis=0, keepdims=True)
        grads[h] = scaled

    def backward(h):
        u_in[h, zh] = u_out[h]
        dl = (u_in[h, 0] + u_in[h, 1] + u_in[h, 2] + u_in[h, 3]) * scales[h]
        dsl = grads[h].astype(BF16)
        don[...] = grads[h].T.astype(BF16)
        dqt[...] = jnp.zeros_like(dqt)

        def body(j, unused):
            dp = mm(kv8[h, j, :, 1].reshape(kc, HD), dsl)
            pr = p_buf[h, j]
            dlog = (pr.astype(F32) * (dp - dl)).astype(BF16)
            dkvb[h, :, j, 1] = mm(pr, don[...]).astype(BF16).reshape(CORES, rows, HD)
            dkvb[h, :, j, 0] = (factor * mm(dlog, q4[h].reshape(nq, HD))).astype(
                BF16).reshape(CORES, rows, HD)
            dqt[...] += mm(kt[h, j], dlog)
            return unused
        lax.fori_loop(0, RING, body, 0)
        dqb[h] = (factor * dqt[...]).T.astype(BF16).reshape(RING, rows, HD)

    def proj(h):
        for t in range(PAIR * RING):
            part = mm(gt[t], attn[h])
            gpb[h, t // 2, 2 * (t % 2):2 * (t % 2) + 2] = part.astype(BF16).reshape(
                2, CORES, wcols, HD)

    def dkv_flow(h):
        c = send(dkvb.at[h, 1 - core], dkvc.at[h], sib)
        yield
        c.wait_recv()
        add_into(dkvb.at[h, core], dkvc.at[h])

        def write(value):
            dk_ref[:, cols(h)] = value[0].astype(BF16)
            dv_ref[:, cols(h)] = value[1].astype(BF16)
        yield from scatter(lambda j, lo, hi: dkvb.at[h, core, j, lo:hi], 2, dkvl.at[h], x, xs,
                           write)

    def dq_flow(h):
        def write(value):
            dq_ref[:, cols(h)] = value.astype(BF16)
        return scatter(lambda j, lo, hi: dqb.at[h, j, lo:hi], rows, dql.at[h], zh, zs, write)

    def gp_flow(h):
        c = send(gpb.at[h, :, :, 1 - core], gpc.at[h], sib)
        yield
        c.wait_recv()
        for j in range(RING):
            add_into(gpb.at[h, j, :, core], gpc.at[h, j])

        def keep(value):
            gpr[h] = value.astype(BF16)
        yield from scatter(lambda j, lo, hi: gpb.at[h, j, lo:hi, core], RING, gpx.at[h], x, xs,
                           keep)

        def final(value):
            gp_ref[:, cols(h)] = value
        yield from scatter(lambda j, lo, hi: gpr.at[h, j, lo:hi], wcols, gpz.at[h], zh, zs, final)

    QZ, KV, WZ = [q_flow(h) for h in H], [kv_flow(h) for h in H], [wz_flow(h) for h in H]
    WX, DZ, OZ = [wx_flow(h) for h in H], [do_flow(h) for h in H], [o_flow(h) for h in H]
    LX = [spread(l_out.at[h], l_in.at[h]) for h in H]
    UX = [spread(u_out.at[h], u_in.at[h]) for h in H]
    DK, DQ, GP = [dkv_flow(h) for h in H], [dq_flow(h) for h in H], [gp_flow(h) for h in H]
    G = g_flow()

    pump(QZ[0], KV[0], WZ[0], G)
    g8[zl, y] = g_ref[...]
    for h in H:
        q4[h, zh] = q_ref[:, cols(h)]
        kv8[h, x, core, 0] = k_ref[:, cols(h)]
        kv8[h, x, core, 1] = v_ref[:, cols(h)]
        wb[h, x, zh, core] = w_ref[:, cols(h)]
    pump(QZ[0], KV[0], QZ[1], KV[1], WZ[0], WZ[1])
    pump(G, KV[0], QZ[0], WZ[0], WX[0], KV[0], QZ[2], KV[2])
    turn(0)
    m0 = logits_pass(0)
    pump(QZ[1], KV[1], WZ[1], WZ[2])
    probs_pass(0, m0)
    pump(LX[0], G, WX[0], QZ[1], KV[1], WZ[1], WX[1], QZ[2], KV[2], KV[1])
    turn(1)
    m1 = logits_pass(1)
    pump(WX[0])
    probs_pass(1, m1)
    pump(LX[1], WZ[2], QZ[2], KV[2], KV[2], LX[0])
    normalise(0, m0)
    pump(OZ[0], WX[0], G)
    grad_attn(0)
    pump(DZ[0], WZ[2], WX[1], WX[2])
    turn(2)
    m2 = logits_pass(2)
    probs_pass(2, m2)
    pump(LX[2], OZ[0], DZ[0], WX[1], WX[1])
    grad_attn(1)
    pump(DZ[1], LX[1])
    normalise(1, m1)
    pump(OZ[1], WX[2], DZ[0])
    row_terms(0)
    pump(UX[0])
    for t in range(PAIR * RING):
        gt[t] = g8[t // RING, t % RING].T
    pump(OZ[0])
    proj(0)
    pump(GP[0], WX[2], WX[2])
    grad_attn(2)
    pump(DZ[2], LX[2])
    normalise(2, m2)
    pump(OZ[2], DZ[1], OZ[1], UX[0])
    backward(0)
    pump(DK[0], DQ[0], GP[0], DZ[1])
    row_terms(1)
    pump(UX[1], OZ[1])
    proj(1)
    pump(GP[1], DZ[2], OZ[2], GP[0], DK[0], DQ[0], UX[1])
    backward(1)
    pump(DK[1], DQ[1], DZ[2])
    row_terms(2)
    pump(UX[2], OZ[2])
    proj(2)
    pump(GP[2], GP[1], GP[0], DK[0], DQ[0], DK[1], DQ[1], UX[2])
    backward(2)
    pump(DK[2], DQ[2], GP[2], GP[1], GP[0], DK[1], DQ[1], DK[0])
    pump(GP[1], GP[2], DK[2], DQ[2], GP[0])
    pump(GP[2], GP[1], DK[2], DQ[2], DK[1])
    pump(GP[2], GP[1], DK[2])
    pump(GP[2])
    for flow in QZ + KV + WZ + WX + DZ + OZ + LX + UX + DK + DQ + GP + [G]:
        for _ in flow:
            pass
    for c in pending:
        c.wait_send()
    assert used[0] <= nsem, used[0]


def local(queries, keys, values, grad_out, proj_weight):
    rows, width = queries.shape
    heads = width // HD
    wcols = proj_weight.shape[1]
    nq, kc = RING * rows, CORES * rows
    nsem = 240

    def vm(*shape, dtype=BF16):
        return pltpu.VMEM(shape, dtype)

    scratch = [
        vm(heads, RING, rows, HD), vm(heads, RING, CORES, 2, rows, HD),
        vm(PAIR, RING, rows, width), vm(PAIR * RING, width, rows),
        vm(heads, RING, RING, CORES, wcols, HD),
        vm(heads, rows, HD), vm(heads, RING, rows, HD),
        vm(heads, HD, nq), vm(heads, RING, HD, kc), vm(heads, RING, HD, kc),
        vm(nq, HD),
        vm(RING, kc, nq, dtype=F32), vm(heads, RING, kc, nq), vm(heads, HD, nq, dtype=F32),
        vm(heads, RING, 1, nq, dtype=F32), vm(heads, 1, nq, dtype=F32),
        vm(heads, 1, nq, dtype=F32), vm(heads, RING, 1, nq, dtype=F32),
        vm(heads, RING, rows, HD), vm(heads, 3, rows, HD),
        vm(HD, nq, dtype=F32), vm(heads, RING, rows, HD), vm(heads, 3, rows, HD),
        vm(heads, CORES, RING, 2, rows, HD), vm(heads, RING, 2, rows, HD),
        vm(heads, 3, 2, rows, HD),
        vm(heads, RING, RING, CORES, wcols, HD), vm(heads, RING, RING, wcols, HD),
        vm(heads, 3, RING, wcols, HD), vm(heads, 3, wcols, HD), vm(heads, RING, wcols, HD),
        pltpu.SemaphoreType.DMA((nsem,)), pltpu.SemaphoreType.DMA((nsem,)),
    ]
    vmem = pl.BlockSpec(memory_space=pltpu.VMEM)

    def body(*refs):
        kernel((rows, heads, wcols, nsem), *refs)

    like = jax.ShapeDtypeStruct((rows, width), BF16)
    dq, dk, dv, gp = pl.pallas_call(
        body,
        out_shape=(like, like, like, jax.ShapeDtypeStruct((wcols, width), F32)),
        in_specs=[vmem] * 5,
        out_specs=(vmem,) * 4,
        scratch_shapes=scratch,
        compiler_params=pltpu.CompilerParams(
            collective_id=0, has_side_effects=True, vmem_limit_bytes=60 * 1024 * 1024),
        name="fused",
    )(queries, keys, values, grad_out, proj_weight.T)
    return dq, dk, dv, gp.T


def solution(mesh):
    spec = P("frame", "space")
    return jax.shard_map(
        local, mesh=mesh, in_specs=(spec,) * 4 + (P("space", "frame"),),
        out_specs=(spec,) * 3 + (P("space", "frame"),), check_vma=False)
```

time: 113 us -> 97.4 us (0.86); the launches traced: 113 us -> 95.7 us
  Pallas kernels: 108 us -> 90.9 us
    pallas_call x1, Pallas kernels: 108 us -> 90.9 us  [local(): pl.pallas_call(body, out_shape=(like, like, like, jax.ShapeDtypeStruct((w...]
where the time goes in v2:
time: 97.4 us; the launch traced here: 95.7 us
  Pallas kernels  90.9 us (93%)
  local copies, waits for them, and re-layouts  4.16 us (4%)
    pallas_call x1, Pallas kernels, local(): pl.pallas_call(body, out_shape=(like, like, like, jax.ShapeDtypeStruct((w...  90.9 us
    unnamed x10, local copies, waits for them, and re-layouts  4.16 us

profile of v2, /device:TPU:8, one launch (start us, length us, event | category | flops | bytes accessed | tf_op | source)
XLA Modules:
  0.0 95.7 jit_solution(4286068572883795453)
XLA Ops:
  0.6 90.9 %fused.1 = (bf16[160,384]{1,0:T(8,128)(2,1)}, bf16[160,384]{1,0:T(8,128)(2,1)}, bf16[160,384]{1,0:T(8,128)(2,1)}, f32[96,384]{1,0:T(8,128)}) custom-call(bf16[160,384]{1,0:T(8,128)(2,1)} %refs_0_.1, bf16[160,384]{1,0:T(8,128)(2,1)} %refs_1_.1, bf16[160,384]{1,0:T(8,128)(2,1)} %refs_2_.1, bf16[160,384]{1,0:T(8,128)(2,1)} %refs_3_.1, bf16[96,384]{1,0:T(8,128)(2,1)} %bitcast.3), custom_call_target="tpu_custom_call" | custom-call | tf_op jit(solution)/shard_map/fused/pallas_call | solution.py:397
  91.6 0.0 copy-start.2
  91.6 1.6 %copy.13 = bf16[160,384]{1,0:T(8,128)(2,1)} copy(bf16[160,384]{1,0:T(8,128)(2,1)} %get-tuple-element.16) | data formatting | bytes 245760
  93.2 0.0 copy-done.2
  93.2 0.0 copy-start.1
  93.2 0.6 copy.14
  93.8 0.3 copy-done.1
  94.1 0.0 copy-start
  94.1 0.6 copy.15
  94.8 0.3 copy-done
  95.1 0.7 copy.16
Async XLA Ops:
  91.6 1.6 %copy-start.2 = (bf16[160,384]{1,0:T(8,128)(2,1)S(1)}, bf16[160,384]{1,0:T(8,128)(2,1)}, u32[]{:S(2)}) copy-start(bf16[160,384]{1,0:T(8,128)(2,1)} %get-tuple-element.17) | copy-start | bytes 368644
  93.2 0.9 copy-start.1
  94.1 1.0 copy-start

commit v3 on v2

--- a/solution.py
+++ b/solution.py
@@ -1,3 +1,4 @@
+import functools
 import math
 
 import jax
@@ -16,13 +17,28 @@
 PAIR = 2
 
 
+ORDER = (
+    "Q01", "Q11", "W01", "W11", "K01", "Q21", "G1", "K11", "W21", "own", "K21", "K02", "Q02",
+    "K12", "Q12", "W02", "K22", "W12", "K03", "K13", "K04", "Q22", "K23", "K14", "K24", "G2",
+    "W22", "Q03", "T0", "L0", "Q13", "W03", "X01", "P0", "W13", "l01", "T1", "L1", "P1", "W23",
+    "G3", "X02", "Q23", "T2", "L2", "l02", "P2", "X03", "N0", "l21", "X11", "l11", "X21", "O01",
+    "X04", "G4", "A0", "D01", "gt", "O02", "X12", "l22", "N2", "l12", "O21", "N1", "O11", "X22",
+    "D02", "X13", "O03", "J0", "Y01", "O22", "X14", "A1", "D11", "X23", "O12", "Y02", "X24", "A2",
+    "D21", "D03", "R0", "u01", "O23", "J2", "Y21", "Y03", "D12", "O13", "J1", "Y22", "Y11", "Y04",
+    "D22", "D13", "R1", "u11", "Y12", "Y23", "u02", "B0", "Y05", "D23", "Y13", "R2", "u21", "V01",
+    "E01", "u12", "B1", "Y24", "Y06", "E11", "Y14", "E02", "V11", "V02", "u22", "B2", "E21",
+    "Y25", "V03", "V21", "V12", "E12", "V22", "Y15", "V04", "V13", "E03", "E22", "V23", "Y26",
+    "E13", "V14", "Y16", "V24", "E23",
+)
+
+
 def mm(a, b):
     return jnp.dot(a, b, preferred_element_type=F32)
 
 
 def kernel(dims, q_ref, k_ref, v_ref, g_ref, w_ref, dq_ref, dk_ref, dv_ref, gp_ref, *scratch):
     rows, heads, wcols, nsem = dims
-    (q4, kv8, g8, gt, wb, da, do4, qt, kt, vt, don, s_buf, p_buf, ot, l_in, u_out, l_out, u_in,
+    (q4, kv8, g8, gt, wb, da, do4, qt, kt, vt, don, dsl, at, s_buf, p_buf, ot, l_in, u_out, l_out, u_in,
      ob, ol, dqt, dqb, dql, dkvb, dkvc, dkvl, gpb, gpc, gpx, gpz, gpr,
      send_sems, recv_sems) = scratch
     width = heads * HD
@@ -174,15 +190,18 @@
             kt[h, j] = kv8[h, j, :, 0].reshape(kc, HD).T
             vt[h, j] = kv8[h, j, :, 1].reshape(kc, HD).T
 
+    tops = {}
+
     def logits_pass(h):
         def body(j, m8):
             sc = mm(kv8[h, j, :, 0].reshape(kc, HD), qt[h])
             s_buf[j] = sc
             return jnp.maximum(m8, jnp.max(sc.reshape(kc // 8, 8, nq), axis=0))
         m8 = lax.fori_loop(0, RING, body, jnp.full((8, nq), -jnp.inf, F32))
-        return jnp.max(m8, axis=0, keepdims=True)
-
-    def probs_pass(h, m):
+        tops[h] = jnp.max(m8, axis=0, keepdims=True)
+
+    def probs_pass(h):
+        m = tops[h]
         ot[h] = jnp.zeros((HD, nq), F32)
 
         def body(j, l8):
@@ -196,19 +215,17 @@
 
     scales = {}
 
-    def normalise(h, m):
+    def normalise(h):
         l_in[h, zh] = l_out[h]
         ls = [l_in[h, j] for j in range(RING)]
         top = jnp.maximum(jnp.maximum(ls[0], ls[1]), jnp.maximum(ls[2], ls[3]))
         total = sum(jnp.exp2(v - top) for v in ls)
-        scales[h] = jnp.exp2(m * c2 - (top + jnp.log2(total)))
+        scales[h] = jnp.exp2(tops[h] * c2 - (top + jnp.log2(total)))
         ob[h] = (ot[h] * scales[h]).T.astype(BF16).reshape(RING, rows, HD)
-
-    attn = {}
 
     def o_flow(h):
         def keep(value):
-            attn[h] = value.astype(BF16)
+            at[h] = value.astype(BF16)
         return scatter(lambda j, lo, hi: ob.at[h, j, lo:hi], rows, ol.at[h], zh, zs, keep)
 
     def grad_attn(h):
@@ -220,25 +237,22 @@
         da[h] = low
         do4[h, zh] = low
 
-    grads = {}
-
     def row_terms(h):
         scaled = do4[h].reshape(nq, HD).astype(F32).T * scales[h]
         u_out[h] = jnp.sum(scaled * ot[h], axis=0, keepdims=True)
-        grads[h] = scaled
+        dsl[h] = scaled.astype(BF16)
+        don[h] = scaled.T.astype(BF16)
 
     def backward(h):
         u_in[h, zh] = u_out[h]
         dl = (u_in[h, 0] + u_in[h, 1] + u_in[h, 2] + u_in[h, 3]) * scales[h]
-        dsl = grads[h].astype(BF16)
-        don[...] = grads[h].T.astype(BF16)
         dqt[...] = jnp.zeros_like(dqt)
 
         def body(j, unused):
-            dp = mm(kv8[h, j, :, 1].reshape(kc, HD), dsl)
+            dp = mm(kv8[h, j, :, 1].reshape(kc, HD), dsl[h])
             pr = p_buf[h, j]
             dlog = (pr.astype(F32) * (dp - dl)).astype(BF16)
-            dkvb[h, :, j, 1] = mm(pr, don[...]).astype(BF16).reshape(CORES, rows, HD)
+            dkvb[h, :, j, 1] = mm(pr, don[h]).astype(BF16).reshape(CORES, rows, HD)
             dkvb[h, :, j, 0] = (factor * mm(dlog, q4[h].reshape(nq, HD))).astype(
                 BF16).reshape(CORES, rows, HD)
             dqt[...] += mm(kt[h, j], dlog)
@@ -248,7 +262,7 @@
 
     def proj(h):
         for t in range(PAIR * RING):
-            part = mm(gt[t], attn[h])
+            part = mm(gt[t], at[h])
             gpb[h, t // 2, 2 * (t % 2):2 * (t % 2) + 2] = part.astype(BF16).reshape(
                 2, CORES, wcols, HD)
 
@@ -291,73 +305,45 @@
     UX = [spread(u_out.at[h], u_in.at[h]) for h in H]
     DK, DQ, GP = [dkv_flow(h) for h in H], [dq_flow(h) for h in H], [gp_flow(h) for h in H]
     G = g_flow()
-
-    pump(QZ[0], KV[0], WZ[0], G)
-    g8[zl, y] = g_ref[...]
+    def own_blocks():
+        g8[zl, y] = g_ref[...]
+        for h in H:
+            q4[h, zh] = q_ref[:, cols(h)]
+            kv8[h, x, core, 0] = k_ref[:, cols(h)]
+            kv8[h, x, core, 1] = v_ref[:, cols(h)]
+            wb[h, x, zh, core] = w_ref[:, cols(h)]
+
+    def turn_g():
+        for t in range(PAIR * RING):
+            gt[t] = g8[t // RING, t % RING].T
+
+    steps = {"own": own_blocks, "gt": turn_g}
+    flows = {"G": g_flow()}
     for h in H:
-        q4[h, zh] = q_ref[:, cols(h)]
-        kv8[h, x, core, 0] = k_ref[:, cols(h)]
-        kv8[h, x, core, 1] = v_ref[:, cols(h)]
-        wb[h, x, zh, core] = w_ref[:, cols(h)]
-    pump(QZ[0], KV[0], QZ[1], KV[1], WZ[0], WZ[1])
-    pump(G, KV[0], QZ[0], WZ[0], WX[0], KV[0], QZ[2], KV[2])
-    turn(0)
-    m0 = logits_pass(0)
-    pump(QZ[1], KV[1], WZ[1], WZ[2])
-    probs_pass(0, m0)
-    pump(LX[0], G, WX[0], QZ[1], KV[1], WZ[1], WX[1], QZ[2], KV[2], KV[1])
-    turn(1)
-    m1 = logits_pass(1)
-    pump(WX[0])
-    probs_pass(1, m1)
-    pump(LX[1], WZ[2], QZ[2], KV[2], KV[2], LX[0])
-    normalise(0, m0)
-    pump(OZ[0], WX[0], G)
-    grad_attn(0)
-    pump(DZ[0], WZ[2], WX[1], WX[2])
-    turn(2)
-    m2 = logits_pass(2)
-    probs_pass(2, m2)
-    pump(LX[2], OZ[0], DZ[0], WX[1], WX[1])
-    grad_attn(1)
-    pump(DZ[1], LX[1])
-    normalise(1, m1)
-    pump(OZ[1], WX[2], DZ[0])
-    row_terms(0)
-    pump(UX[0])
-    for t in range(PAIR * RING):
-        gt[t] = g8[t // RING, t % RING].T
-    pump(OZ[0])
-    proj(0)
-    pump(GP[0], WX[2], WX[2])
-    grad_attn(2)
-    pump(DZ[2], LX[2])
-    normalise(2, m2)
-    pump(OZ[2], DZ[1], OZ[1], UX[0])
-    backward(0)
-    pump(DK[0], DQ[0], GP[0], DZ[1])
-    row_terms(1)
-    pump(UX[1], OZ[1])
-    proj(1)
-    pump(GP[1], DZ[2], OZ[2], GP[0], DK[0], DQ[0], UX[1])
-    backward(1)
-    pump(DK[1], DQ[1], DZ[2])
-    row_terms(2)
-    pump(UX[2], OZ[2])
-    proj(2)
-    pump(GP[2], GP[1], GP[0], DK[0], DQ[0], DK[1], DQ[1], UX[2])
-    backward(2)
-    pump(DK[2], DQ[2], GP[2], GP[1], GP[0], DK[1], DQ[1], DK[0])
-    pump(GP[1], GP[2], DK[2], DQ[2], GP[0])
-    pump(GP[2], GP[1], DK[2], DQ[2], DK[1])
-    pump(GP[2], GP[1], DK[2])
-    pump(GP[2])
-    for flow in QZ + KV + WZ + WX + DZ + OZ + LX + UX + DK + DQ + GP + [G]:
-        for _ in flow:
-            pass
+        for name, make in (("Q", q_flow), ("K", kv_flow), ("W", wz_flow), ("X", wx_flow),
+                           ("D", do_flow), ("O", o_flow), ("V", dkv_flow), ("E", dq_flow),
+                           ("Y", gp_flow)):
+            flows[name + str(h)] = make(h)
+        flows["l" + str(h)] = spread(l_out.at[h], l_in.at[h])
+        flows["u" + str(h)] = spread(u_out.at[h], u_in.at[h])
+        for name, call in (("T", turn), ("L", logits_pass), ("P", probs_pass), ("N", normalise),
+                           ("A", grad_attn), ("R", row_terms), ("B", backward), ("J", proj)):
+            steps[name + str(h)] = functools.partial(call, h)
+    for name in ORDER:
+        if name in steps:
+            steps[name]()
+        else:
+            next(flows[name[:-1]], None)
+    for flow in flows.values():
+        assert next(flow, flow) is flow
     for c in pending:
         c.wait_send()
     assert used[0] <= nsem, used[0]
+
+
+def keep(*refs):
+    for src, dst in zip(refs[:4], refs[4:]):
+        dst[...] = src[...]
 
 
 def local(queries, keys, values, grad_out, proj_weight):
@@ -376,7 +362,7 @@
         vm(heads, RING, RING, CORES, wcols, HD),
         vm(heads, rows, HD), vm(heads, RING, rows, HD),
         vm(heads, HD, nq), vm(heads, RING, HD, kc), vm(heads, RING, HD, kc),
-        vm(nq, HD),
+        vm(heads, nq, HD), vm(heads, HD, nq), vm(heads, rows, HD),
         vm(RING, kc, nq, dtype=F32), vm(heads, RING, kc, nq), vm(heads, HD, nq, dtype=F32),
         vm(heads, RING, 1, nq, dtype=F32), vm(heads, 1, nq, dtype=F32),
         vm(heads, 1, nq, dtype=F32), vm(heads, RING, 1, nq, dtype=F32),
@@ -404,6 +390,13 @@
             collective_id=0, has_side_effects=True, vmem_limit_bytes=60 * 1024 * 1024),
         name="fused",
     )(queries, keys, values, grad_out, proj_weight.T)
+    dq, dk, dv, gp = pl.pallas_call(
+        keep,
+        out_shape=(like, like, like, jax.ShapeDtypeStruct((wcols, width), F32)),
+        in_specs=[vmem] * 4,
+        out_specs=(vmem,) * 4,
+        name="keep",
+    )(dq, dk, dv, gp)
     return dq, dk, dv, gp.T
 
 

time: 97.4 us -> 84.7 us (0.87)
  Pallas kernels: 90.9 us -> 83.3 us
  local copies, waits for them, and re-layouts: 4.16 us -> 0 us
    pallas_call x1, Pallas kernels: 90.9 us -> 81.4 us  [local(): pl.pallas_call(body, out_shape=(like, like, like, jax.ShapeDtypeStruct((w...]
    unnamed x10 -> x0, local copies, waits for them, and re-layouts: 4.16 us -> none
    pallas_call x0 -> x1, Pallas kernels: none -> 1.89 us  [local(): pl.pallas_call(keep, out_shape=(like, like, like, jax.ShapeDtypeStruct((w...]
where the time goes in v3:
time: 84.7 us; the launch traced here: 83.9 us
  Pallas kernels  83.3 us (98%)
    pallas_call x1, Pallas kernels, local(): pl.pallas_call(body, out_shape=(like, like, like, jax.ShapeDtypeStruct((w...  81.4 us
    pallas_call x1, Pallas kernels, local(): pl.pallas_call(keep, out_shape=(like, like, like, jax.ShapeDtypeStruct((w...  1.89 us

profile of v3, /device:TPU:8, one launch (start us, length us, event | category | flops | bytes accessed | tf_op | source)
XLA Modules:
  0.0 83.9 jit_solution(2654875609852444138)
XLA Ops:
  0.6 81.4 %fused.1 = (bf16[160,384]{1,0:T(8,128)(2,1)}, bf16[160,384]{1,0:T(8,128)(2,1)}, bf16[160,384]{1,0:T(8,128)(2,1)}, f32[96,384]{1,0:T(8,128)}) custom-call(bf16[160,384]{1,0:T(8,128)(2,1)} %refs_0_.1, bf16[160,384]{1,0:T(8,128)(2,1)} %refs_1_.1, bf16[160,384]{1,0:T(8,128)(2,1)} %refs_2_.1, bf16[160,384]{1,0:T(8,128)(2,1)} %refs_3_.1, bf16[96,384]{1,0:T(8,128)(2,1)} %bitcast.2), custom_call_target="tpu_custom_call" | custom-call | tf_op jit(solution)/shard_map/fused/pallas_call | solution.py:383
  82.0 1.9 %keep.1 = (bf16[160,384]{1,0:T(8,128)(2,1)}, bf16[160,384]{1,0:T(8,128)(2,1)}, bf16[160,384]{1,0:T(8,128)(2,1)}, f32[96,384]{1,0:T(8,128)}) custom-call(bf16[160,384]{1,0:T(8,128)(2,1)} %get-tuple-element.12.refs_0_, bf16[160,384]{1,0:T(8,128)(2,1)} %get-tuple-element.13.refs_1_, bf16[160,384]{1,0:T(8,128)(2,1)} %get-tuple-element.14.refs_2_, ...), custom_call_target="tpu_custom_call" | custom-call | tf_op jit(solution)/shard_map/keep/pallas_call | solution.py:393

commit v4 on v3

--- a/solution.py
+++ b/solution.py
@@ -18,17 +18,17 @@
 
 
 ORDER = (
-    "Q01", "Q11", "W01", "W11", "K01", "Q21", "G1", "K11", "W21", "own", "K21", "K02", "Q02",
-    "K12", "Q12", "W02", "K22", "W12", "K03", "K13", "K04", "Q22", "K23", "K14", "K24", "G2",
-    "W22", "Q03", "T0", "L0", "Q13", "W03", "X01", "P0", "W13", "l01", "T1", "L1", "P1", "W23",
-    "G3", "X02", "Q23", "T2", "L2", "l02", "P2", "X03", "N0", "l21", "X11", "l11", "X21", "O01",
-    "X04", "G4", "A0", "D01", "gt", "O02", "X12", "l22", "N2", "l12", "O21", "N1", "O11", "X22",
-    "D02", "X13", "O03", "J0", "Y01", "O22", "X14", "A1", "D11", "X23", "O12", "Y02", "X24", "A2",
-    "D21", "D03", "R0", "u01", "O23", "J2", "Y21", "Y03", "D12", "O13", "J1", "Y22", "Y11", "Y04",
-    "D22", "D13", "R1", "u11", "Y12", "Y23", "u02", "B0", "Y05", "D23", "Y13", "R2", "u21", "V01",
-    "E01", "u12", "B1", "Y24", "Y06", "E11", "Y14", "E02", "V11", "V02", "u22", "B2", "E21",
-    "Y25", "V03", "V21", "V12", "E12", "V22", "Y15", "V04", "V13", "E03", "E22", "V23", "Y26",
-    "E13", "V14", "Y16", "V24", "E23",
+    "W01", "K11", "K01", "W11", "G1", "W02", "Q01", "K12", "K02", "W12", "G2", "W21", "K21",
+    "Q11", "W03", "X01", "Q02", "W13", "K13", "Q21", "X11", "K03", "W22", "X02", "Q12", "K22",
+    "K04", "G3", "K14", "Q03", "T0", "L0", "P0", "l01", "W23", "X21", "Q22", "X03", "N0", "O01",
+    "K23", "Q13", "X12", "T1", "L1", "G4", "X04", "A0", "D01", "P1", "Q23", "l11", "X22", "l02",
+    "M0", "O02", "N1", "K24", "X13", "O11", "T2", "L2", "gt", "D02", "X14", "A1", "X23", "D11",
+    "P2", "O03", "J0", "l12", "l21", "N2", "M1", "Y01", "X24", "O12", "A2", "D21", "D03", "R0",
+    "u01", "D12", "Y02", "O21", "O13", "J1", "Y11", "l22", "D22", "M2", "Y03", "D13", "R1", "u11",
+    "Y12", "u02", "O22", "B0", "V01", "D23", "R2", "u21", "Y04", "E01", "Y13", "O23", "J2", "Y21",
+    "u12", "B1", "V11", "Y22", "V02", "Y14", "u22", "E11", "B2", "Y23", "V21", "E02", "V12",
+    "E21", "Y15", "V22", "Y24", "Y05", "V03", "E22", "E12", "V13", "V23", "Y25", "E23", "V14",
+    "V24", "Y16", "Y06", "E03", "E13", "V04", "Y26",
 )
 
 
@@ -38,7 +38,7 @@
 
 def kernel(dims, q_ref, k_ref, v_ref, g_ref, w_ref, dq_ref, dk_ref, dv_ref, gp_ref, *scratch):
     rows, heads, wcols, nsem = dims
-    (q4, kv8, g8, gt, wb, da, do4, qt, kt, vt, don, dsl, at, s_buf, p_buf, ot, l_in, u_out, l_out, u_in,
+    (q4, kv8, g8, gt, wb, da, do4, qt, kt, vt, don, dsl, at, wc, s_buf, p_buf, ot, l_in, u_out, l_out, u_in,
      ob, ol, dqt, dqb, dql, dkvb, dkvc, dkvl, gpb, gpc, gpx, gpz, gpr,
      send_sems, recv_sems) = scratch
     width = heads * HD
@@ -68,6 +68,13 @@
     barrier = pltpu.get_barrier_semaphore()
     for other in partners:
         pl.semaphore_signal(barrier, inc=1, device_id=other, device_id_type=MESH)
+    g8[zl, y] = g_ref[...]
+    for h in range(heads):
+        part = slice(h * HD, (h + 1) * HD)
+        q4[h, zh] = q_ref[:, part]
+        kv8[h, x, core, 0] = k_ref[:, part]
+        kv8[h, x, core, 1] = v_ref[:, part]
+        wb[h, x, zh, core] = w_ref[:, part]
     pl.semaphore_wait(barrier, len(partners))
 
     used = [0]
@@ -190,7 +197,7 @@
             kt[h, j] = kv8[h, j, :, 0].reshape(kc, HD).T
             vt[h, j] = kv8[h, j, :, 1].reshape(kc, HD).T
 
-    tops = {}
+    tops, sums = {}, {}
 
     def logits_pass(h):
         def body(j, m8):
@@ -211,22 +218,55 @@
             ot[h] += mm(vt[h, j], low)
             return l8 + jnp.sum(pr.reshape(kc // 8, 8, nq), axis=0)
         l8 = lax.fori_loop(0, RING, body, jnp.zeros((8, nq), F32))
-        l_out[h] = m * c2 + jnp.log2(jnp.sum(l8, axis=0, keepdims=True))
+        sums[h] = jnp.sum(l8, axis=0, keepdims=True)
+        l_out[h] = m * c2 + jnp.log2(sums[h])
 
     scales = {}
 
-    def normalise(h):
+    def partial_out(h):
+        ob[h] = (ot[h] / sums[h]).T.astype(BF16).reshape(RING, rows, HD)
+
+    def weigh(h):
         l_in[h, zh] = l_out[h]
-        ls = [l_in[h, j] for j in range(RING)]
+        ls = [l_in[h, around(zh, k)] for k in range(RING)]
         top = jnp.maximum(jnp.maximum(ls[0], ls[1]), jnp.maximum(ls[2], ls[3]))
-        total = sum(jnp.exp2(v - top) for v in ls)
-        scales[h] = jnp.exp2(tops[h] * c2 - (top + jnp.log2(total)))
-        ob[h] = (ot[h] * scales[h]).T.astype(BF16).reshape(RING, rows, HD)
+        full = top + jnp.log2(sum(jnp.exp2(v - top) for v in ls))
+        scales[h] = jnp.exp2(tops[h] * c2 - full)
+        table = jnp.concatenate(
+            [jnp.exp2(ls[k] - full) for k in (0, 3, 1)] + [jnp.zeros((5, nq), F32)], axis=0)
+        wc[h] = table.T.reshape(RING, rows, 8)
 
     def o_flow(h):
-        def keep(value):
-            at[h] = value.astype(BF16)
-        return scatter(lambda j, lo, hi: ob.at[h, j, lo:hi], rows, ol.at[h], zh, zs, keep)
+        p, n, o = around(zh, 1), around(zh, 3), around(zh, 2)
+        blk = ob.at[h]
+        land = ol.at[h]
+        lo, hi = slice(0, half), slice(half, rows)
+
+        def w(j, part, k):
+            return wc[h, j, part, k:k + 1]
+
+        def wide(ref):
+            return ref[...].astype(F32)
+        c0 = send(blk.at[o, lo], land.at[0, lo], zs[1])
+        c1 = send(blk.at[o, hi], land.at[0, hi], zs[3])
+        c2_ = send(blk.at[p, hi], land.at[1, hi], zs[1])
+        c3 = send(blk.at[n, lo], land.at[2, lo], zs[3])
+        yield
+        c0.wait_recv()
+        mine = blk.at[p, lo]
+        mine[...] = (wide(mine) * w(p, lo, 0) + wide(land.at[0, lo]) * w(p, lo, 1)).astype(BF16)
+        c4 = send(mine, land.at[1, lo], zs[1])
+        c1.wait_recv()
+        mine = blk.at[n, hi]
+        mine[...] = (wide(mine) * w(n, hi, 0) + wide(land.at[0, hi]) * w(n, hi, 2)).astype(BF16)
+        c5 = send(mine, land.at[2, hi], zs[3])
+        yield
+        for c in (c2_, c3, c4, c5):
+            c.wait_recv()
+        at[h, lo] = (wide(blk.at[zh, lo]) * w(zh, lo, 0) + wide(land.at[1, lo])
+                     + wide(land.at[2, lo]) * w(zh, lo, 2)).astype(BF16)
+        at[h, hi] = (wide(blk.at[zh, hi]) * w(zh, hi, 0) + wide(land.at[1, hi]) * w(zh, hi, 1)
+                     + wide(land.at[2, hi])).astype(BF16)
 
     def grad_attn(h):
         acc = jnp.zeros((rows, HD), F32)
@@ -305,19 +345,11 @@
     UX = [spread(u_out.at[h], u_in.at[h]) for h in H]
     DK, DQ, GP = [dkv_flow(h) for h in H], [dq_flow(h) for h in H], [gp_flow(h) for h in H]
     G = g_flow()
-    def own_blocks():
-        g8[zl, y] = g_ref[...]
-        for h in H:
-            q4[h, zh] = q_ref[:, cols(h)]
-            kv8[h, x, core, 0] = k_ref[:, cols(h)]
-            kv8[h, x, core, 1] = v_ref[:, cols(h)]
-            wb[h, x, zh, core] = w_ref[:, cols(h)]
-
     def turn_g():
         for t in range(PAIR * RING):
             gt[t] = g8[t // RING, t % RING].T
 
-    steps = {"own": own_blocks, "gt": turn_g}
+    steps = {"gt": turn_g}
     flows = {"G": g_flow()}
     for h in H:
         for name, make in (("Q", q_flow), ("K", kv_flow), ("W", wz_flow), ("X", wx_flow),
@@ -326,7 +358,7 @@
             flows[name + str(h)] = make(h)
         flows["l" + str(h)] = spread(l_out.at[h], l_in.at[h])
         flows["u" + str(h)] = spread(u_out.at[h], u_in.at[h])
-        for name, call in (("T", turn), ("L", logits_pass), ("P", probs_pass), ("N", normalise),
+        for name, call in (("T", turn), ("L", logits_pass), ("P", probs_pass), ("N", partial_out), ("M", weigh),
                            ("A", grad_attn), ("R", row_terms), ("B", backward), ("J", proj)):
             steps[name + str(h)] = functools.partial(call, h)
     for name in ORDER:
@@ -363,6 +395,7 @@
         vm(heads, rows, HD), vm(heads, RING, rows, HD),
         vm(heads, HD, nq), vm(heads, RING, HD, kc), vm(heads, RING, HD, kc),
         vm(heads, nq, HD), vm(heads, HD, nq), vm(heads, rows, HD),
+        vm(heads, RING, rows, 8, dtype=F32),
         vm(RING, kc, nq, dtype=F32), vm(heads, RING, kc, nq), vm(heads, HD, nq, dtype=F32),
         vm(heads, RING, 1, nq, dtype=F32), vm(heads, 1, nq, dtype=F32),
         vm(heads, 1, nq, dtype=F32), vm(heads, RING, 1, nq, dtype=F32),

time: 84.7 us -> 77.7 us (0.917)
  Pallas kernels: 83.3 us -> 77 us
    pallas_call x1, Pallas kernels: 81.4 us -> 75.1 us  [local(): pl.pallas_call(body, out_shape=(like, like, like, jax.ShapeDtypeStruct((w...]
where the time goes in v4:
time: 77.7 us; the launch traced here: 77.6 us
  Pallas kernels  77 us (99%)
    pallas_call x1, Pallas kernels, local(): pl.pallas_call(body, out_shape=(like, like, like, jax.ShapeDtypeStruct((w...  75.1 us
    pallas_call x1, Pallas kernels, local(): pl.pallas_call(keep, out_shape=(like, like, like, jax.ShapeDtypeStruct((w...  1.89 us

profile of v4, /device:TPU:8, one launch (start us, length us, event | category | flops | bytes accessed | tf_op | source)
XLA Modules:
  0.0 77.6 jit_solution(7934676784453958187)
XLA Ops:
  0.6 75.1 %fused.1 = (bf16[160,384]{1,0:T(8,128)(2,1)}, bf16[160,384]{1,0:T(8,128)(2,1)}, bf16[160,384]{1,0:T(8,128)(2,1)}, f32[96,384]{1,0:T(8,128)}) custom-call(bf16[160,384]{1,0:T(8,128)(2,1)} %refs_0_.1, bf16[160,384]{1,0:T(8,128)(2,1)} %refs_1_.1, bf16[160,384]{1,0:T(8,128)(2,1)} %refs_2_.1, bf16[160,384]{1,0:T(8,128)(2,1)} %refs_3_.1, bf16[96,384]{1,0:T(8,128)(2,1)} %bitcast.2), custom_call_target="tpu_custom_call" | custom-call | tf_op jit(solution)/shard_map/fused/pallas_call | solution.py:416
  75.7 1.9 %keep.1 = (bf16[160,384]{1,0:T(8,128)(2,1)}, bf16[160,384]{1,0:T(8,128)(2,1)}, bf16[160,384]{1,0:T(8,128)(2,1)}, f32[96,384]{1,0:T(8,128)}) custom-call(bf16[160,384]{1,0:T(8,128)(2,1)} %get-tuple-element.12.refs_0_, bf16[160,384]{1,0:T(8,128)(2,1)} %get-tuple-element.13.refs_1_, bf16[160,384]{1,0:T(8,128)(2,1)} %get-tuple-element.14.refs_2_, ...), custom_call_target="tpu_custom_call" | custom-call | tf_op jit(solution)/shard_map/keep/pallas_call | solution.py:426

commit v5 on v4

--- a/solution.py
+++ b/solution.py
@@ -18,17 +18,17 @@
 
 
 ORDER = (
-    "W01", "K11", "K01", "W11", "G1", "W02", "Q01", "K12", "K02", "W12", "G2", "W21", "K21",
-    "Q11", "W03", "X01", "Q02", "W13", "K13", "Q21", "X11", "K03", "W22", "X02", "Q12", "K22",
-    "K04", "G3", "K14", "Q03", "T0", "L0", "P0", "l01", "W23", "X21", "Q22", "X03", "N0", "O01",
-    "K23", "Q13", "X12", "T1", "L1", "G4", "X04", "A0", "D01", "P1", "Q23", "l11", "X22", "l02",
-    "M0", "O02", "N1", "K24", "X13", "O11", "T2", "L2", "gt", "D02", "X14", "A1", "X23", "D11",
-    "P2", "O03", "J0", "l12", "l21", "N2", "M1", "Y01", "X24", "O12", "A2", "D21", "D03", "R0",
-    "u01", "D12", "Y02", "O21", "O13", "J1", "Y11", "l22", "D22", "M2", "Y03", "D13", "R1", "u11",
-    "Y12", "u02", "O22", "B0", "V01", "D23", "R2", "u21", "Y04", "E01", "Y13", "O23", "J2", "Y21",
-    "u12", "B1", "V11", "Y22", "V02", "Y14", "u22", "E11", "B2", "Y23", "V21", "E02", "V12",
-    "E21", "Y15", "V22", "Y24", "Y05", "V03", "E22", "E12", "V13", "V23", "Y25", "E23", "V14",
-    "V24", "Y16", "Y06", "E03", "E13", "V04", "Y26",
+    "W01", "K11", "W11", "G1", "K01", "K21", "W02", "Q01", "K12", "W12", "W21", "Q11",
+    "G2", "K02", "W03", "X01", "Q02", "K22", "Q21", "W13", "X11", "K13", "W22", "K03", "X02",
+    "Q12", "K14", "K04", "G3", "Q03", "T0", "L0", "P0", "X12", "Q22", "N0", "X03", "l01", "W23",
+    "O01", "X21", "Q13", "T1", "L1", "G4", "X04", "A0", "D01", "K23", "P1", "X13", "N1", "l11",
+    "O11", "Q23", "K24", "l02", "M0", "O02", "X14", "X22", "T2", "A1", "D11", "L2", "D02", "P2",
+    "l12", "M1", "O12", "l21", "N2", "O21", "O03", "X23", "gt", "J0", "Y01", "D12", "X24", "D03",
+    "R0", "A2", "u01", "D21", "O13", "J1", "Y11", "Y02", "l22", "M2", "D13", "R1", "O22", "u11",
+    "Y12", "u02", "D22", "B0", "E01", "Y13", "Y03", "O23", "J2", "Y21", "D23", "R2", "u21", "V01",
+    "u12", "B1", "V11", "E02", "Y22", "Y04", "E11", "u22", "B2", "Y23", "V21", "E21", "V02",
+    "Y05", "Y14", "V12", "Y24", "V22", "E22", "E12", "Y06", "V13", "Y15", "V03", "Y25", "V23",
+    "E03", "E23", "V14", "V04", "Y16", "E13", "Y26", "V24",
 )
 
 
@@ -40,7 +40,7 @@
     rows, heads, wcols, nsem = dims
     (q4, kv8, g8, gt, wb, da, do4, qt, kt, vt, don, dsl, at, wc, s_buf, p_buf, ot, l_in, u_out, l_out, u_in,
      ob, ol, dqt, dqb, dql, dkvb, dkvc, dkvl, gpb, gpc, gpx, gpz, gpr,
-     send_sems, recv_sems) = scratch
+     load_sems, send_sems, recv_sems) = scratch
     width = heads * HD
     nq = RING * rows
     kc = CORES * rows
@@ -68,13 +68,23 @@
     barrier = pltpu.get_barrier_semaphore()
     for other in partners:
         pl.semaphore_signal(barrier, inc=1, device_id=other, device_id_type=MESH)
-    g8[zl, y] = g_ref[...]
+    loads = []
+
+    def load(src, dst):
+        copy = pltpu.make_async_copy(src, dst, load_sems.at[len(loads)])
+        copy.start()
+        loads.append(copy)
+
     for h in range(heads):
         part = slice(h * HD, (h + 1) * HD)
-        q4[h, zh] = q_ref[:, part]
-        kv8[h, x, core, 0] = k_ref[:, part]
-        kv8[h, x, core, 1] = v_ref[:, part]
-        wb[h, x, zh, core] = w_ref[:, part]
+        load(w_ref.at[:, part], wb.at[h, x, zh, core])
+        load(k_ref.at[:, part], kv8.at[h, x, core, 0])
+        load(v_ref.at[:, part], kv8.at[h, x, core, 1])
+        load(q_ref.at[:, part], q4.at[h, zh])
+        if h == 0:
+            load(g_ref, g8.at[zl, y])
+    for copy in loads:
+        copy.wait()
     pl.semaphore_wait(barrier, len(partners))
 
     used = [0]
@@ -158,18 +168,17 @@
     H = range(heads)
 
     def q_flow(h):
-        own = [(q_ref.at[:, cols(h)], q4.at[h, zh])]
+        own = [(q4.at[h, zh], q4.at[h, zh])]
         return gather(own, lambda j: q4.at[h, j], lambda j: q4.at[h, j, 0:half],
                       lambda j: q4.at[h, j, half:rows], zh, zs)
 
     def kv_flow(h):
-        own = [(k_ref.at[:, cols(h)], kv8.at[h, x, core, 0]),
-               (v_ref.at[:, cols(h)], kv8.at[h, x, core, 1])]
+        own = [(kv8.at[h, x, core], kv8.at[h, x, core])]
         return gather(own, lambda j: kv8.at[h, j, core], lambda j: kv8.at[h, j, core, 0],
                       lambda j: kv8.at[h, j, core, 1], x, xs, sib)
 
     def wz_flow(h):
-        own = [(w_ref.at[:, cols(h)], wb.at[h, x, zh, core])]
+        own = [(wb.at[h, x, zh, core], wb.at[h, x, zh, core])]
         return gather(own, lambda j: wb.at[h, x, j, core], lambda j: wb.at[h, x, j, core, 0:hw],
                       lambda j: wb.at[h, x, j, core, hw:wcols], zh, zs)
 
@@ -179,7 +188,7 @@
                       lambda j: wb.at[h, j, 2:4, core], x, xs, sib)
 
     def g_flow():
-        c = send(g_ref, g8.at[zl, y], zsib)
+        c = send(g8.at[zl, y], g8.at[zl, y], zsib)
         yield
         c.wait_recv()
         own = [(g8.at[:, y], g8.at[:, y])]
@@ -405,6 +414,7 @@
         vm(heads, 3, 2, rows, HD),
         vm(heads, RING, RING, CORES, wcols, HD), vm(heads, RING, RING, wcols, HD),
         vm(heads, 3, RING, wcols, HD), vm(heads, 3, wcols, HD), vm(heads, RING, wcols, HD),
+        pltpu.SemaphoreType.DMA((4 * heads + 1,)),
         pltpu.SemaphoreType.DMA((nsem,)), pltpu.SemaphoreType.DMA((nsem,)),
     ]
     vmem = pl.BlockSpec(memory_space=pltpu.VMEM)
@@ -415,8 +425,8 @@
     like = jax.ShapeDtypeStruct((rows, width), BF16)
     dq, dk, dv, gp = pl.pallas_call(
         body,
-        out_shape=(like, like, like, jax.ShapeDtypeStruct((wcols, width), F32)),
-        in_specs=[vmem] * 5,
+        out_shape=(pltpu.VMEM((rows, width), BF16),) * 3 + (pltpu.VMEM((wcols, width), F32),),
+        in_specs=[pl.BlockSpec(memory_space=pl.ANY)] * 5,
         out_specs=(vmem,) * 4,
         scratch_shapes=scratch,
         compiler_params=pltpu.CompilerParams(
@@ -429,7 +439,7 @@
         in_specs=[vmem] * 4,
         out_specs=(vmem,) * 4,
         name="keep",
-    )(dq, dk, dv, gp)
+    )(*(pltpu.with_memory_space_constraint(v, pltpu.VMEM) for v in (dq, dk, dv, gp)))
     return dq, dk, dv, gp.T
 
 

time: 77.7 us -> 75 us (0.965)
  Pallas kernels: 77 us -> 74.1 us
    pallas_call x1, Pallas kernels: 75.1 us -> 73.3 us  [local(): pl.pallas_call(body, out_shape=(pltpu.VMEM((rows, width), BF16),) * 3 + (...]
    pallas_call x1, Pallas kernels: 1.89 us -> 0.83 us  [local(): pl.pallas_call(keep, out_shape=(like, like, like, jax.ShapeDtypeStruct((w...]
where the time goes in v5:
time: 75 us; the launch traced here: 74.8 us
  Pallas kernels  74.1 us (99%)
    pallas_call x1, Pallas kernels, local(): pl.pallas_call(body, out_shape=(pltpu.VMEM((rows, width), BF16),) * 3 + (...  73.3 us

profile of v5, /device:TPU:8, one launch (start us, length us, event | category | flops | bytes accessed | tf_op | source)
XLA Modules:
  0.0 74.8 jit_solution(16770213350091416620)
XLA Ops:
  0.6 73.3 %fused.1 = (bf16[160,384]{1,0:T(8,128)(2,1)S(1)}, bf16[160,384]{1,0:T(8,128)(2,1)S(1)}, bf16[160,384]{1,0:T(8,128)(2,1)S(1)}, f32[96,384]{1,0:T(8,128)S(1)}) custom-call(bf16[160,384]{1,0:T(8,128)(2,1)} %refs_0_.1, bf16[160,384]{1,0:T(8,128)(2,1)} %refs_1_.1, bf16[160,384]{1,0:T(8,128)(2,1)} %refs_2_.1, bf16[160,384]{1,0:T(8,128)(2,1)} %refs_3_.1, ...), custom_call_target="tpu_custom_call" | custom-call | tf_op jit(solution)/shard_map/fused/pallas_call | solution.py:426
  73.9 0.8 %keep.1 = (bf16[160,384]{1,0:T(8,128)(2,1)}, bf16[160,384]{1,0:T(8,128)(2,1)}, bf16[160,384]{1,0:T(8,128)(2,1)}, f32[96,384]{1,0:T(8,128)}) custom-call(bf16[160,384]{1,0:T(8,128)(2,1)S(1)} %get-tuple-element.12.refs_0_, bf16[160,384]{1,0:T(8,128)(2,1)S(1)} %get-tuple-element.13.refs_1_, bf16[160,384]{1,0:T(8,128)(2,1)S(1)} %get-tuple-element.14.refs_2_, ...), custom_call_target="tpu_custom_call" | custom-call | tf_op jit(solution)/shard_map/keep/pallas_call | solution.py:436

commit v6 on v5

--- a/solution.py
+++ b/solution.py
@@ -18,17 +18,17 @@
 
 
 ORDER = (
-    "W01", "K11", "W11", "G1", "K01", "K21", "W02", "Q01", "K12", "W12", "W21", "Q11",
-    "G2", "K02", "W03", "X01", "Q02", "K22", "Q21", "W13", "X11", "K13", "W22", "K03", "X02",
-    "Q12", "K14", "K04", "G3", "Q03", "T0", "L0", "P0", "X12", "Q22", "N0", "X03", "l01", "W23",
-    "O01", "X21", "Q13", "T1", "L1", "G4", "X04", "A0", "D01", "K23", "P1", "X13", "N1", "l11",
-    "O11", "Q23", "K24", "l02", "M0", "O02", "X14", "X22", "T2", "A1", "D11", "L2", "D02", "P2",
-    "l12", "M1", "O12", "l21", "N2", "O21", "O03", "X23", "gt", "J0", "Y01", "D12", "X24", "D03",
-    "R0", "A2", "u01", "D21", "O13", "J1", "Y11", "Y02", "l22", "M2", "D13", "R1", "O22", "u11",
-    "Y12", "u02", "D22", "B0", "E01", "Y13", "Y03", "O23", "J2", "Y21", "D23", "R2", "u21", "V01",
-    "u12", "B1", "V11", "E02", "Y22", "Y04", "E11", "u22", "B2", "Y23", "V21", "E21", "V02",
-    "Y05", "Y14", "V12", "Y24", "V22", "E22", "E12", "Y06", "V13", "Y15", "V03", "Y25", "V23",
-    "E03", "E23", "V14", "V04", "Y16", "E13", "Y26", "V24",
+    "W01", "K11", "K01", "W11", "G1", "W02", "Q01", "K12", "K02", "W12", "G2", "W21", "K21",
+    "Q11", "W03", "X01", "Q02", "W13", "K13", "Q21", "X11", "K03", "W22", "X02", "Q12", "K22",
+    "K04", "G3", "K14", "Q03", "T0", "L0", "P0", "l01", "W23", "X21", "Q22", "X03", "N0", "O01",
+    "K23", "Q13", "X12", "T1", "L1", "G4", "X04", "A0", "D01", "P1", "Q23", "l11", "X22", "l02",
+    "M0", "O02", "N1", "K24", "X13", "O11", "T2", "L2", "gt", "D02", "X14", "A1", "X23", "D11",
+    "P2", "O03", "J0", "l12", "l21", "N2", "M1", "Y01", "X24", "O12", "A2", "D21", "D03", "R0",
+    "u01", "D12", "Y02", "O21", "O13", "J1", "Y11", "l22", "D22", "M2", "Y03", "D13", "R1", "u11",
+    "Y12", "u02", "O22", "B0", "V01", "D23", "R2", "u21", "Y04", "E01", "Y13", "O23", "J2", "Y21",
+    "u12", "B1", "V11", "Y22", "V02", "Y14", "u22", "E11", "B2", "Y23", "V21", "E02", "V12",
+    "E21", "Y15", "V22", "Y24", "Y05", "V03", "E22", "E12", "V13", "V23", "Y25", "E23", "V14",
+    "V24", "Y16", "Y06", "E03", "E13", "V04", "Y26",
 )
 
 
@@ -213,7 +213,7 @@
             sc = mm(kv8[h, j, :, 0].reshape(kc, HD), qt[h])
             s_buf[j] = sc
             return jnp.maximum(m8, jnp.max(sc.reshape(kc // 8, 8, nq), axis=0))
-        m8 = lax.fori_loop(0, RING, body, jnp.full((8, nq), -jnp.inf, F32))
+        m8 = lax.fori_loop(0, RING, body, jnp.full((8, nq), -jnp.inf, F32), unroll=True)
         tops[h] = jnp.max(m8, axis=0, keepdims=True)
 
     def probs_pass(h):
@@ -226,7 +226,7 @@
             p_buf[h, j] = low
             ot[h] += mm(vt[h, j], low)
             return l8 + jnp.sum(pr.reshape(kc // 8, 8, nq), axis=0)
-        l8 = lax.fori_loop(0, RING, body, jnp.zeros((8, nq), F32))
+        l8 = lax.fori_loop(0, RING, body, jnp.zeros((8, nq), F32), unroll=True)
         sums[h] = jnp.sum(l8, axis=0, keepdims=True)
         l_out[h] = m * c2 + jnp.log2(sums[h])
 
@@ -306,7 +306,7 @@
                 BF16).reshape(CORES, rows, HD)
             dqt[...] += mm(kt[h, j], dlog)
             return unused
-        lax.fori_loop(0, RING, body, 0)
+        lax.fori_loop(0, RING, body, 0, unroll=True)
         dqb[h] = (factor * dqt[...]).T.astype(BF16).reshape(RING, rows, HD)
 
     def proj(h):

time: 75 us -> 73.9 us (0.985)
  Pallas kernels: 74.1 us -> 73.1 us
    pallas_call x1, Pallas kernels: 73.3 us -> 72.3 us  [local(): pl.pallas_call(body, out_shape=(pltpu.VMEM((rows, width), BF16),) * 3 + (...]
where the time goes in v6:
time: 73.9 us; the launch traced here: 73.8 us
  Pallas kernels  73.1 us (99%)
    pallas_call x1, Pallas kernels, local(): pl.pallas_call(body, out_shape=(pltpu.VMEM((rows, width), BF16),) * 3 + (...  72.3 us

profile of v6, /device:TPU:8, one launch (start us, length us, event | category | flops | bytes accessed | tf_op | source)
XLA Modules:
  0.0 73.8 jit_solution(3396627241297710748)
XLA Ops:
  0.6 72.3 %fused.1 = (bf16[160,384]{1,0:T(8,128)(2,1)S(1)}, bf16[160,384]{1,0:T(8,128)(2,1)S(1)}, bf16[160,384]{1,0:T(8,128)(2,1)S(1)}, f32[96,384]{1,0:T(8,128)S(1)}) custom-call(bf16[160,384]{1,0:T(8,128)(2,1)} %refs_0_.1, bf16[160,384]{1,0:T(8,128)(2,1)} %refs_1_.1, bf16[160,384]{1,0:T(8,128)(2,1)} %refs_2_.1, bf16[160,384]{1,0:T(8,128)(2,1)} %refs_3_.1, ...), custom_call_target="tpu_custom_call" | custom-call | tf_op jit(solution)/shard_map/fused/pallas_call | solution.py:426
  73.0 0.8 %keep.1 = (bf16[160,384]{1,0:T(8,128)(2,1)}, bf16[160,384]{1,0:T(8,128)(2,1)}, bf16[160,384]{1,0:T(8,128)(2,1)}, f32[96,384]{1,0:T(8,128)}) custom-call(bf16[160,384]{1,0:T(8,128)(2,1)S(1)} %get-tuple-element.12.refs_0_, bf16[160,384]{1,0:T(8,128)(2,1)S(1)} %get-tuple-element.13.refs_1_, bf16[160,384]{1,0:T(8,128)(2,1)S(1)} %get-tuple-element.14.refs_2_, ...), custom_call_target="tpu_custom_call" | custom-call | tf_op jit(solution)/shard_map/keep/pallas_call | solution.py:436

commit v7 on v6

--- a/solution.py
+++ b/solution.py
@@ -18,17 +18,17 @@
 
 
 ORDER = (
-    "W01", "K11", "K01", "W11", "G1", "W02", "Q01", "K12", "K02", "W12", "G2", "W21", "K21",
-    "Q11", "W03", "X01", "Q02", "W13", "K13", "Q21", "X11", "K03", "W22", "X02", "Q12", "K22",
-    "K04", "G3", "K14", "Q03", "T0", "L0", "P0", "l01", "W23", "X21", "Q22", "X03", "N0", "O01",
-    "K23", "Q13", "X12", "T1", "L1", "G4", "X04", "A0", "D01", "P1", "Q23", "l11", "X22", "l02",
-    "M0", "O02", "N1", "K24", "X13", "O11", "T2", "L2", "gt", "D02", "X14", "A1", "X23", "D11",
-    "P2", "O03", "J0", "l12", "l21", "N2", "M1", "Y01", "X24", "O12", "A2", "D21", "D03", "R0",
-    "u01", "D12", "Y02", "O21", "O13", "J1", "Y11", "l22", "D22", "M2", "Y03", "D13", "R1", "u11",
-    "Y12", "u02", "O22", "B0", "V01", "D23", "R2", "u21", "Y04", "E01", "Y13", "O23", "J2", "Y21",
-    "u12", "B1", "V11", "Y22", "V02", "Y14", "u22", "E11", "B2", "Y23", "V21", "E02", "V12",
-    "E21", "Y15", "V22", "Y24", "Y05", "V03", "E22", "E12", "V13", "V23", "Y25", "E23", "V14",
-    "V24", "Y16", "Y06", "E03", "E13", "V04", "Y26",
+    "W01", "K11", "W11", "K01", "G1", "W02", "Q01", "K21", "W12", "K02", "W21", "G2", "K12",
+    "Q11", "W03", "X01", "Q02", "Q21", "W13", "K03", "X11", "K13", "W22", "K04", "Q12", "X02",
+    "K14", "K22", "Q03", "T0", "G3", "L0", "P0", "X12", "N0", "l01", "W23", "O01", "X21", "Q22",
+    "X03", "Q13", "T1", "L1", "P1", "N1", "l11", "O11", "K23", "X13", "X04", "G4", "A0", "D01",
+    "l02", "X22", "K24", "X14", "Q23", "M0", "A1", "O02", "D11", "T2", "L2", "l12", "P2", "M1",
+    "l21", "O12", "X23", "N2", "D02", "gt", "O21", "O03", "X24", "J0", "Y01", "A2", "D21", "O13",
+    "D12", "J1", "D03", "l22", "R0", "Y11", "M2", "u01", "O22", "Y02", "D22", "Y12", "D13", "R1",
+    "u11", "O23", "J2", "Y21", "Y03", "u02", "B0", "V01", "Y13", "D23", "R2", "u21", "E01", "Y22",
+    "u12", "B1", "V11", "E11", "Y04", "Y14", "Y23", "u22", "B2", "V21", "V12", "E21", "V02",
+    "Y24", "Y05", "V22", "E02", "E12", "V13", "Y15", "V03", "E22", "Y25", "V23", "E13", "Y06",
+    "E03", "V14", "V04", "Y16", "E23", "V24", "Y26",
 )
 
 

time: 73.9 us -> 72.3 us (0.978); the launches traced: 73.8 us -> 71.3 us
  Pallas kernels: 73.1 us -> 70.6 us
    pallas_call x1, Pallas kernels: 72.3 us -> 69.8 us  [local(): pl.pallas_call(body, out_shape=(pltpu.VMEM((rows, width), BF16),) * 3 + (...]
where the time goes in v7:
time: 72.3 us; the launch traced here: 71.3 us
  Pallas kernels  70.6 us (98%)
    pallas_call x1, Pallas kernels, local(): pl.pallas_call(body, out_shape=(pltpu.VMEM((rows, width), BF16),) * 3 + (...  69.8 us

profile of v7, /device:TPU:8, one launch (start us, length us, event | category | flops | bytes accessed | tf_op | source)
XLA Modules:
  0.0 71.3 jit_solution(18040394210096594895)
XLA Ops:
  0.6 69.8 %fused.1 = (bf16[160,384]{1,0:T(8,128)(2,1)S(1)}, bf16[160,384]{1,0:T(8,128)(2,1)S(1)}, bf16[160,384]{1,0:T(8,128)(2,1)S(1)}, f32[96,384]{1,0:T(8,128)S(1)}) custom-call(bf16[160,384]{1,0:T(8,128)(2,1)} %refs_0_.1, bf16[160,384]{1,0:T(8,128)(2,1)} %refs_1_.1, bf16[160,384]{1,0:T(8,128)(2,1)} %refs_2_.1, bf16[160,384]{1,0:T(8,128)(2,1)} %refs_3_.1, ...), custom_call_target="tpu_custom_call" | custom-call | tf_op jit(solution)/shard_map/fused/pallas_call | solution.py:426
  70.4 0.8 %keep.1 = (bf16[160,384]{1,0:T(8,128)(2,1)}, bf16[160,384]{1,0:T(8,128)(2,1)}, bf16[160,384]{1,0:T(8,128)(2,1)}, f32[96,384]{1,0:T(8,128)}) custom-call(bf16[160,384]{1,0:T(8,128)(2,1)S(1)} %get-tuple-element.12.refs_0_, bf16[160,384]{1,0:T(8,128)(2,1)S(1)} %get-tuple-element.13.refs_1_, bf16[160,384]{1,0:T(8,128)(2,1)S(1)} %get-tuple-element.14.refs_2_, ...), custom_call_target="tpu_custom_call" | custom-call | tf_op jit(solution)/shard_map/keep/pallas_call | solution.py:436
